TPU v7x, 512 devices: a whole 4x8x8 slice. The times are simulated.
512 devices in a mesh: row: 64 (over y, z_hi, core), col: 8 (over z_lo, x).
Axes of the slice: x: 4, y: 8, z: 8 (z_hi: 4, z_lo: 2; z = z_hi * 2 + z_lo), core: 2. Of those that a mesh axis runs over, the one named last changes fastest.
Arguments:
- grad_x: float32 [6144, 4096], P('row', 'col'), may hold values from -6 to 6
- grad_y: float32 [6144, 4096], P('row', 'col'), may hold values from -6 to 6
- weight_x: float32 [6144, 4096], P('row', 'col'), may hold values from 0.1 to 10
- weight_y: float32 [6144, 4096], P('row', 'col'), may hold values from 0.1 to 10
- anchor: float32 [6144, 4096], P('row', 'col'), may hold values from 0.02 to 0.5
- prior: float32 [6144, 4096], P('row', 'col'), may hold values from -6 to 6
Outputs:
- heights: float32 [6144, 4096], P('row', 'col')
- residual: float32 [6144, 4096], P('row', 'col')
All inputs are finite; a program needn't handle non-finite values.
Results may differ from a plain program's by a relative error of at most 0.0002.
Values sent between devices are 32-bit elements; how exact they have to be, the bound alone decides.
A program may use at most 64 MiB of HBM per device.

v0:
```python
import jax
import jax.numpy as jnp
from jax import lax
from jax.sharding import PartitionSpec as P

ITERS = 3
SWEEPS = 4


damping = 2.0 / 3.0


def shifted(block, axis, distance):
    devices = range(lax.axis_size(axis))
    route = [(i - distance, i) for i in devices if i - distance in devices]
    return lax.ppermute(block, axis, route)


def with_halo(array, sides, width):
    for axis, dim in sides:
        size, length = (lax.axis_size(axis), array.shape[dim])
        up = [(i, (i + 1) % size) for i in range(size - 1)]
        down = [(j, i) for i, j in up]
        last = lax.slice_in_dim(array, length - width, length, axis=dim)
        first = lax.slice_in_dim(array, 0, width, axis=dim)
        before = lax.ppermute(last, axis, up)
        after = lax.ppermute(first, axis, down)
        array = jnp.concatenate([before, array, after], axis=dim)
    return array


def block_view(field):
    return field.reshape(field.shape[0] // 4, 4, field.shape[1] // 4, 4)


def sweep(padded, coarse, coeffs):
    centre = padded[1:-1, 1:-1]
    beside = coeffs[0] * padded[1:-1, :-2] + coeffs[1] * padded[1:-1, 2:]
    beside = beside + coeffs[2] * padded[:-2, 1:-1] + coeffs[3] * padded[2:, 1:-1]
    return (1.0 - damping) * centre + damping * coeffs[4] * (coarse + beside)


def agreement_sum(resid, smooth):
    return lax.psum(jnp.sum(resid * smooth), ("row", "col"))


def local(grad_x, grad_y, weight_x, weight_y, anchor, prior):
    tile_rows, tile_cols = grad_x.shape
    row_ids = lax.axis_index("row") * tile_rows + lax.broadcasted_iota(jnp.int32, grad_x.shape, 0)
    col_ids = lax.axis_index("col") * tile_cols + lax.broadcasted_iota(jnp.int32, grad_x.shape, 1)
    right_w = jnp.where(col_ids < tile_cols * lax.axis_size("col") - 1, weight_x, jnp.float32(0.0))
    down_w = jnp.where(row_ids < tile_rows * lax.axis_size("row") - 1, weight_y, jnp.float32(0.0))
    flux_x = right_w * grad_x
    flux_y = down_w * grad_y
    left_edge = shifted(jnp.stack([right_w[:, -1], flux_x[:, -1]]), "col", 1)
    top_edge = shifted(jnp.stack([down_w[-1, :], flux_y[-1, :]]), "row", 1)
    left_w = jnp.concatenate([left_edge[0][:, None], right_w[:, :-1]], 1)
    left_flux = jnp.concatenate([left_edge[1][:, None], flux_x[:, :-1]], 1)
    up_w = jnp.concatenate([top_edge[0][None, :], down_w[:-1, :]], 0)
    up_flux = jnp.concatenate([top_edge[1][None, :], flux_y[:-1, :]], 0)
    source = anchor * prior + left_flux - flux_x + up_flux - flux_y
    diag = anchor + left_w + right_w + up_w + down_w
    inverse = 1.0 / diag
    c_left = block_view(left_w)[:, :, :, 0].sum(1)
    c_right = block_view(right_w)[:, :, :, 3].sum(1)
    c_up = block_view(up_w)[:, 0, :, :].sum(2)
    c_down = block_view(down_w)[:, 3, :, :].sum(2)
    c_anchor = block_view(anchor).sum((1, 3))
    c_inverse = 1.0 / (c_anchor + c_left + c_right + c_up + c_down)
    coeffs = jnp.stack([c_left, c_right, c_up, c_down, c_inverse])

    def precondition(resid):
        coarse = block_view(resid).sum((1, 3))
        level = damping * coeffs[4] * coarse
        for turn in range(SWEEPS - 1):
            padded = with_halo(level, (("row", 0), ("col", 1)), 1)
            level = sweep(padded, coarse, coeffs)
        spread = jnp.broadcast_to(level[:, None, :, None], (level.shape[0], 4, level.shape[1], 4))
        return inverse * resid + spread.reshape(resid.shape)

    heights = jnp.zeros_like(source)
    residual = source
    smooth = precondition(residual)
    agree = agreement_sum(residual, smooth)
    direction = smooth
    for step in range(ITERS):
        operate_padded = with_halo(direction, (("row", 0), ("col", 1)), 1)
        beside = left_w * operate_padded[1:-1, :-2] + right_w * operate_padded[1:-1, 2:]
        beside = beside + up_w * operate_padded[:-2, 1:-1] + down_w * operate_padded[2:, 1:-1]
        image = diag * direction - beside
        alpha = agree / lax.psum(jnp.sum(direction * image), ("row", "col"))
        heights = heights + alpha * direction
        residual = residual - alpha * image
        if step + 1 < ITERS:
            smooth = precondition(residual)
            agree_next = agreement_sum(residual, smooth)
            direction = smooth + agree_next / agree * direction
            agree = agree_next
    return (heights, residual)


def solution(mesh):
    return jax.shard_map(
        local,
        mesh=mesh,
        in_specs=(
            P("row", "col"),
            P("row", "col"),
            P("row", "col"),
            P("row", "col"),
            P("row", "col"),
            P("row", "col"),
        ),
        out_specs=(P("row", "col"), P("row", "col")),
        check_vma=False,
    )
```

profile of v0, /device:TPU:1, one launch (start us, length us, event | category | flops | bytes accessed | tf_op | source)
XLA Modules:
  0.0 889.1 jit_solution(11664116397091542020)
XLA Ops:
  1.9 3.9 collective-permute-start
  7.0 6.6 collective-permute-start.1
  13.7 7.8 reshape.44
  21.5 7.8 reshape.42
  29.4 4.9 slice_reduce_fusion
  36.2 7.8 reshape.40
  44.0 3.3 reduce_sum.126
  47.6 7.8 reshape.41
  55.4 3.3 slice_reduce_fusion.1
  58.9 7.8 reshape.43
  68.8 7.8 reshape.45
  76.6 3.3 reduce_sum.131
  84.3 6.2 collective-permute-done.3
  90.6 3.1 collective-permute-start.4
  95.0 3.2 collective-permute-done.5
  98.3 3.4 collective-permute-start.6
  103.6 3.8 collective-permute-done.7
  107.5 3.0 collective-permute-start.8
  111.9 3.2 collective-permute-done.9
  115.1 4.1 collective-permute-start.10
  121.2 4.2 collective-permute-done.11
  125.5 4.9 collective-permute-start.12
  131.7 3.2 collective-permute-done.13
  135.0 3.5 broadcast_in_dim.12
  138.5 6.6 reshape.46
  145.3 3.9 collective-permute-start.14
  151.2 4.5 collective-permute-done.15
  155.8 3.7 collective-permute-start.16
  160.9 3.6 collective-permute-done.17
  165.3 107.0 %all-reduce = (f32[]{:T(128)}, f32[]{:T(128)}) all-reduce(f32[]{:T(128)} %get-tuple-element.3, f32[]{:T(128)} %get-tuple-element.2), channel_id=1, replica_groups=mesh['row'=64,'col'=8] {'row','col'}, use_global_device_ids=true, to_apply=%region_7.8 | all-reduce | flops 2 | bytes 16 | tf_op jit(solution)/shard_map/psum | solution.py:44
  273.7 7.8 reshape.47
  281.6 3.3 reduce_sum.134
  289.3 3.8 collective-permute-done.19
  297.3 3.2 collective-permute-done.21
  300.6 3.4 collective-permute-start.22
  305.9 3.8 collective-permute-done.23
  312.8 5.2 collective-permute-done.25
  318.1 3.7 collective-permute-start.26
  323.7 4.5 collective-permute-done.27
  328.3 5.7 collective-permute-start.28
  335.3 3.2 collective-permute-done.29
  338.6 3.5 broadcast_in_dim.13
  342.1 6.6 reshape.48
  349.4 107.7 %psum.44 = f32[]{:T(128)} all-reduce(f32[]{:T(128)} %multiply_reduce_fusion.3), channel_id=1, replica_groups=mesh['row'=64,'col'=8] {'row','col'}, use_global_device_ids=true, to_apply=%region_12.13 | all-reduce | flops 1 | bytes 8 | tf_op jit(solution)/shard_map/psum | solution.py:44
  462.9 3.9 collective-permute-done.31
  471.1 3.6 collective-permute-done.33
  475.6 103.8 %psum.45 = f32[]{:T(128)} all-reduce(f32[]{:T(128)} %get-tuple-element.8), channel_id=1, replica_groups=mesh['row'=64,'col'=8] {'row','col'}, use_global_device_ids=true, to_apply=%region_14.15 | all-reduce | flops 1 | bytes 8 | tf_op jit(solution)/shard_map/psum | solution.py:91
  580.8 7.8 reshape.49
  588.6 3.3 reduce_sum.137
  596.4 3.8 collective-permute-done.35
  604.5 3.2 collective-permute-done.37
  607.7 3.4 collective-permute-start.38
  613.1 3.8 collective-permute-done.39
  620.0 5.1 collective-permute-done.41
  625.2 3.7 collective-permute-start.42
  630.8 4.5 collective-permute-done.43
  635.4 5.7 collective-permute-start.44
  642.4 3.2 collective-permute-done.45
  645.7 3.5 broadcast_in_dim.26
  649.2 6.6 reshape.50
  656.5 107.7 %psum.46 = f32[]{:T(128)} all-reduce(f32[]{:T(128)} %multiply_reduce_fusion.1), channel_id=1, replica_groups=mesh['row'=64,'col'=8] {'row','col'}, use_global_device_ids=true, to_apply=%region_17.18 | all-reduce | flops 1 | bytes 8 | tf_op jit(solution)/shard_map/psum | solution.py:44
  770.0 3.9 collective-permute-done.47
  778.3 3.6 collective-permute-done.49
  782.7 103.6 %psum.47 = f32[]{:T(128)} all-reduce(f32[]{:T(128)} %get-tuple-element.6), channel_id=1, replica_groups=mesh['row'=64,'col'=8] {'row','col'}, use_global_device_ids=true, to_apply=%region_19.20 | all-reduce | flops 1 | bytes 8 | tf_op jit(solution)/shard_map/psum | solution.py:91
  (140 shorter events, 79.9 us)
Async XLA Ops:
  1.9 45.4 %collective-permute-start = (f32[2,96]{1,0:T(2,128)S(1)}, f32[2,96]{1,0:T(2,128)S(1)}, u32[]{:S(2)}, u32[]{:S(2)}) collective-permute-start(f32[2,96]{1,0:T(2,128)S(1)} %pad_maximum_fusion.117), channel_id=1, source_target_pairs={{0,1},{1,2},{2,3},{3,4},{4,5},{5,6},{6,7},{8,9},{9,10},{10,11},{11... | collective-permute-start | bytes 2312 | tf_op jit(solution)/shard_map/ppermute | solution.py:16
  7.0 51.8 %collective-permute-start.1 = (f32[2,512]{1,0:T(2,128)S(1)}, f32[2,512]{1,0:T(2,128)S(1)}, u32[]{:S(2)}, u32[]{:S(2)}) collective-permute-start(f32[2,512]{1,0:T(2,128)S(1)} %pad_maximum_fusion.116), channel_id=1, source_target_pairs={{0,8},{8,16},{16,24},{24,32},{32,40},{40,48},{48,56},{56,64},{64,7... | collective-permute-start | bytes 12296 | tf_op jit(solution)/shard_map/ppermute | solution.py:16
  21.5 14.6 %copy-start = (f32[96,512]{1,0:T(8,128)S(1)}, f32[96,512]{1,0:T(8,128)}, u32[]{:S(2)}) copy-start(f32[96,512]{1,0:T(8,128)} %param.10) | copy-start | bytes 589828
  55.4 13.2 %copy-start.1 = (f32[96,512]{1,0:T(8,128)S(1)}, f32[96,512]{1,0:T(8,128)}, u32[]{:S(2)}) copy-start(f32[96,512]{1,0:T(8,128)} %param.11) | copy-start | bytes 589828
  79.9 4.3 collective-permute-start.2
  81.8 8.6 collective-permute-start.3
  90.6 4.4 collective-permute-start.4
  93.7 4.5 collective-permute-start.5
  98.3 5.3 collective-permute-start.6
  101.7 5.8 collective-permute-start.7
  107.5 4.3 collective-permute-start.8
  110.5 4.5 collective-permute-start.9
  115.1 6.1 collective-permute-start.10
  119.3 6.2 collective-permute-start.11
  125.5 6.2 collective-permute-start.12
  130.4 4.5 collective-permute-start.13
  145.3 5.9 collective-permute-start.14
  149.3 6.5 collective-permute-start.15
  155.8 5.1 collective-permute-start.16
  159.6 4.9 collective-permute-start.17
  284.9 4.4 collective-permute-start.18
  287.3 5.8 collective-permute-start.19
  293.2 4.1 collective-permute-start.20
  296.0 4.5 collective-permute-start.21
  300.6 5.3 collective-permute-start.22
  304.0 5.8 collective-permute-start.23
  309.9 2.9 collective-permute-start.24
  311.5 6.5 collective-permute-start.25
  318.1 5.6 collective-permute-start.26
  321.8 6.4 collective-permute-start.27
  328.3 7.0 collective-permute-start.28
  334.0 4.5 collective-permute-start.29
  458.5 4.4 collective-permute-start.30
  461.0 5.8 collective-permute-start.31
  466.9 4.3 collective-permute-start.32
  469.8 4.9 collective-permute-start.33
  591.9 4.4 collective-permute-start.34
  594.4 5.8 collective-permute-start.35
  600.3 4.2 collective-permute-start.36
  603.2 4.5 collective-permute-start.37
  607.7 5.3 collective-permute-start.38
  611.1 5.8 collective-permute-start.39
  617.0 2.9 collective-permute-start.40
  618.6 6.4 collective-permute-start.41
  625.2 5.6 collective-permute-start.42
  628.8 6.4 collective-permute-start.43
  635.4 7.0 collective-permute-start.44
  641.1 4.5 collective-permute-start.45
  765.7 4.4 collective-permute-start.46
  768.1 5.8 collective-permute-start.47
  774.0 4.3 collective-permute-start.48
  776.9 4.9 collective-permute-start.49
where the time goes:
time: 892 us; the launch traced here: 889 us
  blocking collectives  530 us (59%)
  starting transfers between devices  128 us (14%)
  local copies, waits for them, and re-layouts  94.4 us (11%)
  waiting for transfers between devices  94.2 us (11%)
  other arithmetic  34.4 us (4%)
    psum x3, blocking collectives, agreement_sum(): return lax.psum(jnp.sum(resid * smooth), ('row', 'col'))  322 us
    psum x2, blocking collectives, local(): alpha = agree / lax.psum(jnp.sum(direction * image), ('row', 'col'))  207 us
    ppermute x24, waiting for transfers between devices, with_halo(): after = lax.ppermute(first, axis, down)  94.2 us
    ppermute x24, starting transfers between devices, with_halo(): before = lax.ppermute(last, axis, up)  78.3 us
    reshape x8, local copies, waits for them, and re-layouts, block_view(): return field.reshape(field.shape[0] // 4, 4, field.shape[1] // 4, 4)  62.8 us
    ppermute x24, starting transfers between devices, with_halo(): after = lax.ppermute(first, axis, down)  39 us
    reshape x3, local copies, waits for them, and re-layouts, precondition(): return inverse * resid + spread.reshape(resid.shape)  19.9 us
  transfers between devices with their start and end apart: 50, of which 24 were waited for; matrix products, arithmetic and copies ran while one was open for 5% of the time, Pallas kernels for 0%

commit v1 on v0

v1 whole, which is shorter than its diff:
```python
import functools

import jax
import jax.numpy as jnp
from jax import lax
from jax.experimental import pallas as pl
from jax.experimental.pallas import tpu as pltpu
from jax.sharding import PartitionSpec as P

MESH = pl.DeviceIdType.MESH
F = jnp.float32
OMEGA = 2.0 / 3.0

SPLIT = dict(y=8, zh=4, core=2, zl=2, x=4)


def iota(shape, dim):
    return lax.broadcasted_iota(jnp.int32, shape, dim)


def pick(masks, values):
    out = values[-1]
    for mask, value in zip(masks[:-1][::-1], values[:-1][::-1]):
        out = jnp.where(mask, value, out)
    return out


def lane_gather(x, index):
    return jnp.take_along_axis(x, index, axis=1, mode="promise_in_bounds")


def deal(parts, lane):
    low = [(lane & 3) == q for q in range(4)]
    block = [(lane >> 5) == v for v in range(4)]
    moved = []
    for d in range(4):
        merged = pick([low[(v + d) & 3] for v in range(4)], parts)
        moved.append(lane_gather(merged, 4 * (lane & 31) + (((lane >> 5) + d) & 3)))
    return [pick(block, [moved[(s - v) & 3] for v in range(4)]) for s in range(4)]


def undeal(planes, lane):
    low = [(lane & 3) == q for q in range(4)]
    block = [(lane >> 5) == v for v in range(4)]
    moved = []
    for d in range(4):
        merged = pick(block, [planes[(v + d) & 3] for v in range(4)])
        moved.append(lane_gather(merged, 32 * (((lane & 3) - d) & 3) + (lane >> 2)))
    return [pick(low, [moved[(q - v) & 3] for q in range(4)]) for v in range(4)]


def roll(x, shift, axis):
    shift = shift % x.shape[axis]
    return pltpu.roll(x, shift, axis) if shift else x


def kernel(split, *refs):
    ny, nzh, ncore, nzl, nx = (split[k] for k in ("y", "zh", "core", "zl", "x"))
    nrow, ncol = ny * nzh * ncore, nzl * nx
    inputs, refs = refs[:6], refs[6:]
    heights_ref, resid_ref = refs[:2]
    (raw, rw_ref, dw_ref, diag_ref, inv_ref, lw_ref, uw_ref, r0_ref, u_ref, w_ref,
     s0h, s0v, g0h, g0v, s1h, s1u, s1d, g1h, g1v, sh, su, sd, gh, gv,
     part, slots_a, slots_b, slots_c, done,
     in_sem, out_sem, s0_sem, g0_sem, sx_sem, gx_sem, sr_sem, gr_sem) = refs[2:]

    row, col = lax.axis_index("row"), lax.axis_index("col")
    up, down = lax.rem(row + nrow - 1, nrow), lax.rem(row + 1, nrow)
    left, right = lax.rem(col + ncol - 1, ncol), lax.rem(col + 1, ncol)
    neighbours = [(up, col), (up, left), (up, right), (down, col), (down, left), (down, right), (row, left), (row, right)]

    y, zh, core = row // (nzh * ncore), lax.rem(row // ncore, nzh), lax.rem(row, ncore)
    zl, x = col // nx, lax.rem(col, nx)
    z = zh * nzl + zl

    def device(y, z, core, x):
        return ((y * nzh + z // nzl) * ncore + core, lax.rem(z, nzl) * nx + x)

    na, nb, nc = nx * ncore, ny, nzh * nzl
    me_a = x * ncore + core

    def partner_a(k):
        other = lax.rem(me_a + k, na)
        return device(y, z, lax.rem(other, ncore), other // ncore)

    def partner_b(k):
        return device(lax.rem(y + k, ny), z, core, x)

    def partner_c(k):
        return device(y, lax.rem(z + k, nc), core, x)

    loads = [
        [pltpu.make_async_copy(src.at[:, 128 * v:128 * v + 128], raw.at[k, v], in_sem.at[k, v]) for v in range(4)]
        for k, src in enumerate(inputs)
    ]
    for k in (2, 3, 0, 1, 4, 5):
        for copy in loads[k]:
            copy.start()

    partners = neighbours + [partner_a(k) for k in range(1, na)]
    partners += [partner_b(k) for k in range(1, nb)] + [partner_c(k) for k in range(1, nc)]
    barrier = pltpu.get_barrier_semaphore()
    for who in partners:
        pl.semaphore_signal(barrier, inc=1, device_id=who, device_id_type=MESH)

    shape = (24, 128)
    lane, sub = iota(shape, 1), iota(shape, 0)
    lane8, sub8 = iota((8, 128), 1), iota((8, 128), 0)

    def load(k):
        for copy in loads[k]:
            copy.wait()
        out = []
        for t in range(4):
            parts = [raw[k, v, pl.ds(t, 24, stride=4), :] for v in range(4)]
            out += deal(parts, lane)
        return out

    def pack_cols(planes, source, base, out=None):
        for t, plane in enumerate(planes):
            moved = roll(plane, base + t - source, 1)
            out = moved if out is None else jnp.where(lane == base + t, moved, out)
        return out

    def pack_rows(planes, source, base, out=None):
        for s, plane in enumerate(planes):
            tile = plane[8 * (source // 8):8 * (source // 8) + 8]
            moved = roll(tile, base + s - source % 8, 0)
            out = moved if out is None else jnp.where(sub8 == base + s, moved, out)
        return out

    rw = load(2)
    at_end = jnp.logical_and(lane == 127, col == ncol - 1)
    for t in range(4):
        rw[4 * t + 3] = jnp.where(at_end, 0.0, rw[4 * t + 3])
    dw = load(3)
    at_end = jnp.logical_and(sub == 23, row == nrow - 1)
    for s in range(4):
        dw[12 + s] = jnp.where(at_end, 0.0, dw[12 + s])
    fx = [a * b for a, b in zip(rw, load(0))]
    fy = [a * b for a, b in zip(dw, load(1))]
    s0h[...] = pack_cols(fx[3::4], 127, 124, pack_cols(rw[3::4], 127, 120))
    s0v[...] = pack_rows(fy[12:], 23, 4, pack_rows(dw[12:], 23, 0))
    pl.semaphore_wait(barrier, len(partners))
    phase0 = [
        pltpu.make_async_remote_copy(s0h, g0h, s0_sem.at[0], g0_sem.at[0], device_id=(row, right), device_id_type=MESH),
        pltpu.make_async_remote_copy(s0v, g0v, s0_sem.at[1], g0_sem.at[1], device_id=(down, col), device_id_type=MESH),
    ]
    for copy in phase0:
        copy.start()
    for k in range(16):
        rw_ref[k] = rw[k]
        dw_ref[k] = dw[k]
    anchor = load(4)
    prior = load(5)
    source = [anchor[k] * prior[k] - fx[k] - fy[k] for k in range(16)]
    for copy in phase0:
        copy.wait()

    def shift_left_edge(planes, halo, base):
        return [jnp.where(lane == 0, roll(halo, -(base + t), 1), roll(planes[t], 1, 1)) for t in range(4)]

    def shift_up_edge(planes, halo, base):
        return [
            jnp.where(sub == 0, jnp.broadcast_to(halo[base + s:base + s + 1], shape), roll(planes[s], 1, 0))
            for s in range(4)
        ]

    halo = g0h[...]
    lw0 = shift_left_edge(rw[3::4], halo, 120)
    fl0 = shift_left_edge(fx[3::4], halo, 124)
    halo = g0v[...]
    uw0 = shift_up_edge(dw[12:], halo, 0)
    fu0 = shift_up_edge(fy[12:], halo, 4)
    lw = [lw0[k // 4] if k % 4 == 0 else rw[k - 1] for k in range(16)]
    fl = [fl0[k // 4] if k % 4 == 0 else fx[k - 1] for k in range(16)]
    uw = [uw0[k] if k < 4 else dw[k - 4] for k in range(16)]
    fu = [fu0[k] if k < 4 else fy[k - 4] for k in range(16)]
    diag = [anchor[k] + lw[k] + rw[k] + uw[k] + dw[k] for k in range(16)]
    resid = [source[k] + fl[k] + fu[k] for k in range(16)]
    inv = [1.0 / d for d in diag]
    for k in range(16):
        diag_ref[k] = diag[k]
        inv_ref[k] = inv[k]
        r0_ref[k] = resid[k]
    for k in range(4):
        lw_ref[k] = lw0[k]
        uw_ref[k] = uw0[k]

    def total(planes):
        while len(planes) > 1:
            planes = [a + b for a, b in zip(planes[::2], planes[1::2])]
        return planes[0]

    c_right, c_down = total(rw[3::4]), total(dw[12:])
    c_inv = 1.0 / (total(anchor) + total(lw0) + c_right + total(uw0) + c_down)

    def pack(coarse, planes, h_ref, u_ref, d_ref):
        h, u, d = coarse, coarse[:8], coarse[16:]
        if planes is not None:
            h = pack_cols(planes[3::4], 127, 120, pack_cols(planes[0::4], 0, 4, h))
            u = pack_rows(planes[:4], 0, 4, u)
            d = pack_rows(planes[12:], 23, 0, d)
        h_ref[...] = h
        u_ref[...] = u
        d_ref[...] = d

    def exchange(h, u, d, got_h, got_v, send, recv):
        plan = [(u, got_v.at[0], (up, col)), (u, got_v.at[1], (up, left)), (u, got_v.at[2], (up, right))]
        plan += [(d, got_v.at[3], (down, col)), (d, got_v.at[4], (down, left)), (d, got_v.at[5], (down, right))]
        plan += [(h, got_h.at[0], (row, left)), (h, got_h.at[1], (row, right))]
        plan = [plan[k] for k in (1, 2, 4, 5, 0, 3, 6, 7)]
        out = [
            pltpu.make_async_remote_copy(src, dst, send.at[k], recv.at[k], device_id=who, device_id_type=MESH)
            for k, (src, dst, who) in enumerate(plan)
        ]
        for copy in out:
            copy.start()
        return out

    coarse = total(resid)
    pack(c_right, inv, s1h.at[0], s1u.at[0], s1d.at[0])
    pack(c_down, None, s1h.at[1], s1u.at[1], s1d.at[1])
    pack(c_inv, None, s1h.at[2], s1u.at[2], s1d.at[2])
    pack(coarse, resid, s1h.at[3], s1u.at[3], s1d.at[3])
    copies = exchange(s1h, s1u, s1d, g1h, g1v, sx_sem.at[0], gx_sem.at[0])

    def assemble(own, h, v):
        side = jnp.where(lane < 64, h[0], h[1])
        ring = jnp.where(jnp.logical_or(lane < 4, lane >= 124), side, 0.0)
        below = jnp.where(sub8 < 4, v[0], v[3])
        corner = jnp.where(
            lane8 < 4,
            jnp.where(sub8 < 4, v[1], v[4]),
            jnp.where(lane8 >= 124, jnp.where(sub8 < 4, v[2], v[5]), 0.0),
        )
        ends = jnp.where(sub8 < 4, v[3], v[0])
        ext = jnp.concatenate(
            [jnp.concatenate([own, ring], axis=1), jnp.concatenate([below, corner], axis=1)], axis=0
        )
        return ext, side, ends

    def field(h, v, f=None):
        if f is None:
            return [h[k] for k in range(2)], [v[k] for k in range(6)]
        return [h[k, f] for k in range(2)], [v[k, f] for k in range(6)]

    for copy in copies:
        copy.wait()
    cr, inv_side, inv_ends = assemble(c_right, *field(g1h, g1v, 0))
    cd, _, _ = assemble(c_down, *field(g1h, g1v, 1))
    ci, _, _ = assemble(c_inv, *field(g1h, g1v, 2))
    scale = OMEGA * ci
    a_right, a_left = scale * cr, scale * roll(cr, 1, 1)
    a_down, a_up = scale * cd, scale * roll(cd, 1, 0)

    def smooth(own, h, v):
        ext, side, ends = assemble(own, h, v)
        start = scale * ext
        level = start
        for turn in range(3):
            beside = a_left * roll(level, 1, 1) + a_right * roll(level, -1, 1)
            beside = beside + a_up * roll(level, 1, 0) + a_down * roll(level, -1, 0)
            level = (1.0 - OMEGA) * level + (start + beside)
        e_side, e_ends = level[:24, 128:], level[24:, :128]
        e_side = jnp.where(
            lane < 64, jnp.broadcast_to(e_side[:, 0:1], shape), jnp.broadcast_to(e_side[:, 127:128], shape)
        )
        e_ends = jnp.where(
            sub8 < 4, jnp.broadcast_to(e_ends[7:8], (8, 128)), jnp.broadcast_to(e_ends[0:1], (8, 128))
        )
        return level[:24, :128], inv_side * side + e_side, inv_ends * ends + e_ends

    def operate(v, side, ends, emit):
        west = [jnp.where(lane == 0, roll(side, -(120 + t), 1), roll(v[4 * t + 3], 1, 1)) for t in range(4)]
        east = [jnp.where(lane == 127, roll(side, 127 - (4 + t), 1), roll(v[4 * t], -1, 1)) for t in range(4)]
        north = [
            jnp.where(sub == 0, jnp.broadcast_to(ends[s:s + 1], shape), roll(v[12 + s], 1, 0)) for s in range(4)
        ]
        south = [
            jnp.where(sub == 23, jnp.broadcast_to(ends[4 + s:5 + s], shape), roll(v[s], -1, 0)) for s in range(4)
        ]
        for k in range(16):
            t, s = k // 4, k % 4
            beside = (lw_ref[t] * west[t]) if s == 0 else (rw_ref[k - 1] * v[k - 1])
            beside = beside + rw_ref[k] * (east[t] if s == 3 else v[k + 1])
            beside = beside + ((uw_ref[s] * north[s]) if t == 0 else (dw_ref[k - 4] * v[k - 4]))
            beside = beside + dw_ref[k] * (south[s] if t == 3 else v[k + 4])
            emit(k, diag_ref[k] * v[k] - beside)

    def dot(a, b):
        return total([a[k] * b[k] for k in range(16)])

    sums = {}
    got = field(g1h, g1v, 3)
    source, sides, ends = [resid], None, None
    images, fields = [], []
    for j in range(3):
        if j:
            for copy in copies:
                copy.wait()
            got = field(gh.at[j - 1], gv.at[j - 1])
        level, new_side, new_ends = smooth(coarse, *got)
        if j == 0:
            v = [inv_ref[k] * resid[k] + level for k in range(16)]
            side, ends = new_side, new_ends
        else:
            v = [inv_ref[k] * images[-1][k] + level - fields[-1][k] for k in range(16)]
            side, ends = new_side - side, new_ends - ends
        image = [None] * 16

        def emit(k, value):
            image[k] = value

        operate(v, side, ends, emit)
        for k in range(16):
            u_ref[j, k] = v[k]
            w_ref[j, k] = image[k]
        fields.append(v)
        images.append(image)
        if j < 2:
            coarse = total(image)
            pack(coarse, image, sh.at[j], su.at[j], sd.at[j])
            copies = exchange(sh.at[j], su.at[j], sd.at[j], gh.at[j], gv.at[j], sx_sem.at[j + 1], gx_sem.at[j + 1])
        sums["g", j] = dot(resid, v)
        for i in range(j + 1):
            sums[i, j] = dot(images[i], v)

    order = [("g", 0), ("g", 1), ("g", 2), (0, 0), (0, 1), (0, 2), (1, 1), (1, 2), (2, 2)]
    sums_row = jnp.zeros((1, 128), F)
    lane1 = iota((1, 128), 1)
    for k, name in enumerate(order):
        x8 = sums[name]
        x8 = x8[:8] + x8[8:16] + x8[16:]
        for shift in (64, 32, 16, 8):
            x8 = x8 + roll(x8, shift, 1)
        one = jnp.sum(x8, axis=0, keepdims=True)
        sums_row = jnp.where((lane1 >> 3) == k, one, sums_row)

    base = 0
    for slots, count, me, partner in (
        (slots_a, na, me_a, partner_a), (slots_b, nb, y, partner_b), (slots_c, nc, z, partner_c)
    ):
        part[base] = sums_row
        copies = []
        for k in range(1, count):
            copies.append(pltpu.make_async_remote_copy(
                part.at[base], slots.at[k], sr_sem.at[base, k], gr_sem.at[base, k],
                device_id=partner(k), device_id_type=MESH,
            ))
            copies[-1].start()
        for copy in copies:
            copy.wait()
        sums_row = total_any([sums_row] + [slots[k] for k in range(1, count)])
        base += 1

    for shift in (4, 2, 1):
        sums_row = sums_row + roll(sums_row, -shift, 1)
    value = {
        name: jnp.broadcast_to(sums_row[:, 8 * k:8 * k + 1], (1, 128)) for k, name in enumerate(order)
    }
    g0, g1, g2 = (value["g", j] for j in range(3))
    a00, a01, a02 = value[0, 0], value[0, 1], value[0, 2]
    l10, l20 = a01 / a00, a02 / a00
    d1, t12 = value[1, 1] - l10 * a01, value[1, 2] - l10 * a02
    l21 = t12 / d1
    d2 = value[2, 2] - l20 * a02 - l21 * t12
    y1 = g1 - l10 * g0
    y2 = g2 - l20 * g0 - l21 * y1
    c2 = y2 / d2
    c1 = y1 / d1 - l21 * c2
    c0 = g0 / a00 - l10 * c1 - l20 * c2
    c = [jnp.broadcast_to(v, shape) for v in (c0, c1, c2)]

    stores = []
    for n, out_ref in enumerate((heights_ref, resid_ref)):
        for t in range(4):
            planes = []
            for k in range(4 * t, 4 * t + 4):
                if n == 0:
                    planes.append(c[0] * u_ref[0, k] + c[1] * u_ref[1, k] + c[2] * u_ref[2, k])
                else:
                    planes.append(r0_ref[k] - (c[0] * w_ref[0, k] + c[1] * w_ref[1, k] + c[2] * w_ref[2, k]))
            for v, value in enumerate(undeal(planes, lane)):
                done[n, v, pl.ds(t, 24, stride=4), :] = value
        for v in range(4):
            stores.append(
                pltpu.make_async_copy(done.at[n, v], out_ref.at[:, 128 * v:128 * v + 128], out_sem.at[n, v])
            )
            stores[-1].start()
    for copy in stores:
        copy.wait()


def total_any(values):
    while len(values) > 1:
        rest = values[len(values) // 2 * 2:]
        values = [a + b for a, b in zip(values[::2], values[1::2])] + rest
    return values[0]


def solution(mesh, split=SPLIT):
    na, nb, nc = split["x"] * split["core"], split["y"], split["zh"] * split["zl"]

    def step(*args):
        rows, cols = args[0].shape
        assert (rows, cols) == (96, 512)
        tile, planes = pltpu.VMEM((24, 128), F), pltpu.VMEM((16, 24, 128), F)
        dma = pltpu.SemaphoreType.DMA
        most = max(na, nb, nc)
        out = pl.pallas_call(
            functools.partial(kernel, split),
            out_shape=[jax.ShapeDtypeStruct((rows, cols), F)] * 2,
            in_specs=[pl.BlockSpec(memory_space=pltpu.HBM)] * 6,
            out_specs=[pl.BlockSpec(memory_space=pltpu.HBM)] * 2,
            scratch_shapes=[
                pltpu.VMEM((6, 4, rows, 128), F),
                planes, planes, planes, planes,
                pltpu.VMEM((4, 24, 128), F), pltpu.VMEM((4, 24, 128), F),
                planes,
                pltpu.VMEM((3, 16, 24, 128), F), pltpu.VMEM((3, 16, 24, 128), F),
                tile, pltpu.VMEM((8, 128), F), tile, pltpu.VMEM((8, 128), F),
                pltpu.VMEM((4, 24, 128), F), pltpu.VMEM((4, 8, 128), F), pltpu.VMEM((4, 8, 128), F),
                pltpu.VMEM((2, 4, 24, 128), F), pltpu.VMEM((6, 4, 8, 128), F),
                pltpu.VMEM((2, 24, 128), F), pltpu.VMEM((2, 8, 128), F), pltpu.VMEM((2, 8, 128), F),
                pltpu.VMEM((2, 2, 24, 128), F), pltpu.VMEM((2, 6, 8, 128), F),
                pltpu.VMEM((3, 1, 128), F),
                pltpu.VMEM((na, 1, 128), F), pltpu.VMEM((nb, 1, 128), F), pltpu.VMEM((nc, 1, 128), F),
                pltpu.VMEM((2, 4, rows, 128), F),
                dma((6, 4)), dma((2, 4)), dma((2,)), dma((2,)), dma((3, 8)), dma((3, 8)), dma((3, most)), dma((3, most)),
            ],
            compiler_params=pltpu.CompilerParams(collective_id=0, has_side_effects=True),
        )(*args)
        return tuple(out)

    return jax.shard_map(
        step,
        mesh=mesh,
        in_specs=(P("row", "col"),) * 6,
        out_specs=(P("row", "col"),) * 2,
        check_vma=False,
    )
```

time: 892 us -> 52.5 us (0.06)
  blocking collectives: 530 us -> 0 us
  starting transfers between devices: 128 us -> 0 us
  waiting for transfers between devices: 94.2 us -> 0 us
  local copies, waits for them, and re-layouts: 94.4 us -> 2.34 us
  Pallas kernels: 0 us -> 49 us
  other arithmetic: 34.4 us -> 0 us
    psum x5 -> x0, blocking collectives: 530 us -> none  [the longest x3 322 us: agreement_sum(): return lax.psum(jnp.sum(resid * smooth), ('row', 'col'))]
    ppermute x50 -> x0, starting transfers between devices: 128 us -> none  [the longest x24 78.3 us: with_halo(): before = lax.ppermute(last, axis, up)]
    ppermute x50 -> x0, waiting for transfers between devices: 94.2 us -> none  [the longest x24 94.2 us: with_halo(): after = lax.ppermute(first, axis, down)]
    reshape x11 -> x0, local copies, waits for them, and re-layouts: 82.7 us -> none  [the longest x8 62.8 us: block_view(): return field.reshape(field.shape[0] // 4, 4, field.shape[1] // 4, 4)]
    pallas_call x0 -> x1, Pallas kernels: none -> 49 us  [step(): pl.pallas_call(functools.partial(kernel, split), out_shape=[jax.ShapeDtyp...]
    reduce_sum x13 -> x0, other arithmetic: 29.1 us -> none  [the longest x3 9.84 us: precondition(): coarse = block_view(resid).sum((1, 3))]
    broadcast_in_dim x3 -> x0, local copies, waits for them, and re-layouts: 10.5 us -> none  [precondition(): jnp.broadcast_to(level[:, None, :, None], (level.shape[0], 4, level.shape...]
  transfers between devices with their start and end apart: 50 -> 0, of which waited for: 24 -> 0; matrix products, arithmetic and copies ran while one was open for 5% -> 0% of each run, Pallas kernels for 0% -> 0%
where the time goes in v1:
time: 52.5 us; the launch traced here: 52 us
  Pallas kernels  49 us (93%)
  local copies, waits for them, and re-layouts  2.34 us (4%)
  between operations  0.65 us (1%)
    pallas_call x1, Pallas kernels, step(): pl.pallas_call(functools.partial(kernel, split), out_shape=[jax.ShapeDtyp...  49 us
    unnamed x4, local copies, waits for them, and re-layouts  2.34 us

profile of v1, /device:TPU:1, one launch (start us, length us, event | category | flops | bytes accessed | tf_op | source)
XLA Modules:
  0.0 52.0 jit_solution(2054768439187782715)
XLA Ops:
  0.6 49.0 %shard_map.77 = (f32[96,512]{1,0:T(8,128)}, f32[96,512]{1,0:T(8,128)}) custom-call(f32[96,512]{1,0:T(8,128)} %refs_0_.1, f32[96,512]{1,0:T(8,128)} %refs_1_.1, f32[96,512]{1,0:T(8,128)} %refs_2_.1, f32[96,512]{1,0:T(8,128)} %refs_3_.1, f32[96,512]{1,0:T(8,128)} %refs_4_.1, f32[96,512]{1,0:T(8,128)} %refs_5_.1), custom_call_target="tpu_custom_call" | custom-call | tf_op jit(solution)/shard_map/pallas_call | solution.py:411
  49.7 0.0 copy-start
  49.7 1.7 %copy.10 = f32[96,512]{1,0:T(8,128)} copy(f32[96,512]{1,0:T(8,128)} %get-tuple-element.4) | data formatting | bytes 393216
  51.3 0.0 copy-done
  51.3 0.7 %copy.11 = f32[96,512]{1,0:T(8,128)} copy(f32[96,512]{1,0:T(8,128)S(1)} %copy-done) | data formatting | bytes 393216
Async XLA Ops:
  49.7 1.7 %copy-start = (f32[96,512]{1,0:T(8,128)S(1)}, f32[96,512]{1,0:T(8,128)}, u32[]{:S(2)}) copy-start(f32[96,512]{1,0:T(8,128)} %get-tuple-element.5) | copy-start | bytes 589828

commit v2 on v1

--- a/solution.py
+++ b/solution.py
@@ -58,11 +58,11 @@
     ny, nzh, ncore, nzl, nx = (split[k] for k in ("y", "zh", "core", "zl", "x"))
     nrow, ncol = ny * nzh * ncore, nzl * nx
     inputs, refs = refs[:6], refs[6:]
-    heights_ref, resid_ref = refs[:2]
-    (raw, rw_ref, dw_ref, diag_ref, inv_ref, lw_ref, uw_ref, r0_ref, u_ref, w_ref,
-     s0h, s0v, g0h, g0v, s1h, s1u, s1d, g1h, g1v, sh, su, sd, gh, gv,
-     part, slots_a, slots_b, slots_c, done,
-     in_sem, out_sem, s0_sem, g0_sem, sx_sem, gx_sem, sr_sem, gr_sem) = refs[2:]
+    r0_ref, u_ref, w_ref, c_ref = refs[:4]
+    (raw, rw_ref, dw_ref, diag_ref, inv_ref, lw_ref, uw_ref,
+     sent0, got0, s1h, s1u, s1d, got1, sh, su, sd, got,
+     part, slots_a, slots_b, slots_c,
+     in_sem, s0_sem, g0_sem, sx_sem, gx_sem, sr_sem, gr_sem) = refs[4:]
 
     row, col = lax.axis_index("row"), lax.axis_index("col")
     up, down = lax.rem(row + nrow - 1, nrow), lax.rem(row + 1, nrow)
@@ -90,7 +90,7 @@
         return device(y, lax.rem(z + k, nc), core, x)
 
     loads = [
-        [pltpu.make_async_copy(src.at[:, 128 * v:128 * v + 128], raw.at[k, v], in_sem.at[k, v]) for v in range(4)]
+        [pltpu.make_async_copy(src.at[:, 128 * v:128 * v + 128], raw.at[k, v], in_sem.at[k]) for v in range(4)]
         for k, src in enumerate(inputs)
     ]
     for k in (2, 3, 0, 1, 4, 5):
@@ -103,13 +103,15 @@
     for who in partners:
         pl.semaphore_signal(barrier, inc=1, device_id=who, device_id_type=MESH)
 
+    def finish(ref, sem):
+        pltpu.make_async_copy(ref, ref, sem).wait()
+
     shape = (24, 128)
     lane, sub = iota(shape, 1), iota(shape, 0)
     lane8, sub8 = iota((8, 128), 1), iota((8, 128), 0)
 
     def load(k):
-        for copy in loads[k]:
-            copy.wait()
+        finish(raw.at[k], in_sem.at[k])
         out = []
         for t in range(4):
             parts = [raw[k, v, pl.ds(t, 24, stride=4), :] for v in range(4)]
@@ -139,23 +141,20 @@
         dw[12 + s] = jnp.where(at_end, 0.0, dw[12 + s])
     fx = [a * b for a, b in zip(rw, load(0))]
     fy = [a * b for a, b in zip(dw, load(1))]
-    s0h[...] = pack_cols(fx[3::4], 127, 124, pack_cols(rw[3::4], 127, 120))
-    s0v[...] = pack_rows(fy[12:], 23, 4, pack_rows(dw[12:], 23, 0))
+    sent0[:3] = pack_cols(fx[3::4], 127, 124, pack_cols(rw[3::4], 127, 120)).reshape(3, 8, 128)
+    sent0[3] = pack_rows(fy[12:], 23, 4, pack_rows(dw[12:], 23, 0))
     pl.semaphore_wait(barrier, len(partners))
-    phase0 = [
-        pltpu.make_async_remote_copy(s0h, g0h, s0_sem.at[0], g0_sem.at[0], device_id=(row, right), device_id_type=MESH),
-        pltpu.make_async_remote_copy(s0v, g0v, s0_sem.at[1], g0_sem.at[1], device_id=(down, col), device_id_type=MESH),
-    ]
-    for copy in phase0:
-        copy.start()
+    for part0, who in ((pl.ds(0, 3), (row, right)), (pl.ds(3, 1), (down, col))):
+        pltpu.make_async_remote_copy(
+            sent0.at[part0], got0.at[part0], s0_sem, g0_sem, device_id=who, device_id_type=MESH
+        ).start()
     for k in range(16):
         rw_ref[k] = rw[k]
         dw_ref[k] = dw[k]
     anchor = load(4)
     prior = load(5)
     source = [anchor[k] * prior[k] - fx[k] - fy[k] for k in range(16)]
-    for copy in phase0:
-        copy.wait()
+    finish(got0, g0_sem)
 
     def shift_left_edge(planes, halo, base):
         return [jnp.where(lane == 0, roll(halo, -(base + t), 1), roll(planes[t], 1, 1)) for t in range(4)]
@@ -166,10 +165,10 @@
             for s in range(4)
         ]
 
-    halo = g0h[...]
+    halo = got0[:3].reshape(shape)
     lw0 = shift_left_edge(rw[3::4], halo, 120)
     fl0 = shift_left_edge(fx[3::4], halo, 124)
-    halo = g0v[...]
+    halo = got0[3]
     uw0 = shift_up_edge(dw[12:], halo, 0)
     fu0 = shift_up_edge(fy[12:], halo, 4)
     lw = [lw0[k // 4] if k % 4 == 0 else rw[k - 1] for k in range(16)]
@@ -201,29 +200,24 @@
             h = pack_cols(planes[3::4], 127, 120, pack_cols(planes[0::4], 0, 4, h))
             u = pack_rows(planes[:4], 0, 4, u)
             d = pack_rows(planes[12:], 23, 0, d)
-        h_ref[...] = h
-        u_ref[...] = u
-        d_ref[...] = d
-
-    def exchange(h, u, d, got_h, got_v, send, recv):
-        plan = [(u, got_v.at[0], (up, col)), (u, got_v.at[1], (up, left)), (u, got_v.at[2], (up, right))]
-        plan += [(d, got_v.at[3], (down, col)), (d, got_v.at[4], (down, left)), (d, got_v.at[5], (down, right))]
-        plan += [(h, got_h.at[0], (row, left)), (h, got_h.at[1], (row, right))]
-        plan = [plan[k] for k in (1, 2, 4, 5, 0, 3, 6, 7)]
-        out = [
-            pltpu.make_async_remote_copy(src, dst, send.at[k], recv.at[k], device_id=who, device_id_type=MESH)
-            for k, (src, dst, who) in enumerate(plan)
-        ]
-        for copy in out:
-            copy.start()
-        return out
+        h_ref[...] = h.reshape(3, 8, 128)
+        u_ref[0] = u
+        d_ref[0] = d
+
+    def exchange(h, u, d, got, n, send, recv):
+        plan = [(u, 1, (up, left)), (u, 2, (up, right)), (d, 4, (down, left)), (d, 5, (down, right))]
+        plan += [(u, 0, (up, col)), (d, 3, (down, col))]
+        plan = [(src, got.at[pl.ds((6 + slot) * n, n)], who) for src, slot, who in plan]
+        plan += [(h, got.at[pl.ds(0, 3 * n)], (row, left)), (h, got.at[pl.ds(3 * n, 3 * n)], (row, right))]
+        for src, dst, who in plan:
+            pltpu.make_async_remote_copy(src, dst, send, recv, device_id=who, device_id_type=MESH).start()
 
     coarse = total(resid)
-    pack(c_right, inv, s1h.at[0], s1u.at[0], s1d.at[0])
-    pack(c_down, None, s1h.at[1], s1u.at[1], s1d.at[1])
-    pack(c_inv, None, s1h.at[2], s1u.at[2], s1d.at[2])
-    pack(coarse, resid, s1h.at[3], s1u.at[3], s1d.at[3])
-    copies = exchange(s1h, s1u, s1d, g1h, g1v, sx_sem.at[0], gx_sem.at[0])
+    pack(c_right, inv, s1h.at[pl.ds(0, 3)], s1u.at[pl.ds(0, 1)], s1d.at[pl.ds(0, 1)])
+    pack(c_down, None, s1h.at[pl.ds(3, 3)], s1u.at[pl.ds(1, 1)], s1d.at[pl.ds(1, 1)])
+    pack(c_inv, None, s1h.at[pl.ds(6, 3)], s1u.at[pl.ds(2, 1)], s1d.at[pl.ds(2, 1)])
+    pack(coarse, resid, s1h.at[pl.ds(9, 3)], s1u.at[pl.ds(3, 1)], s1d.at[pl.ds(3, 1)])
+    exchange(s1h, s1u, s1d, got1, 4, sx_sem.at[0], gx_sem.at[0])
 
     def assemble(own, h, v):
         side = jnp.where(lane < 64, h[0], h[1])
@@ -240,16 +234,14 @@
         )
         return ext, side, ends
 
-    def field(h, v, f=None):
-        if f is None:
-            return [h[k] for k in range(2)], [v[k] for k in range(6)]
-        return [h[k, f] for k in range(2)], [v[k, f] for k in range(6)]
-
-    for copy in copies:
-        copy.wait()
-    cr, inv_side, inv_ends = assemble(c_right, *field(g1h, g1v, 0))
-    cd, _, _ = assemble(c_down, *field(g1h, g1v, 1))
-    ci, _, _ = assemble(c_inv, *field(g1h, g1v, 2))
+    def field(ref, n, f):
+        h = [ref[pl.ds(3 * (n * k + f), 3)].reshape(shape) for k in range(2)]
+        return h, [ref[n * (6 + k) + f] for k in range(6)]
+
+    finish(got1, gx_sem.at[0])
+    cr, inv_side, inv_ends = assemble(c_right, *field(got1, 4, 0))
+    cd, _, _ = assemble(c_down, *field(got1, 4, 1))
+    ci, _, _ = assemble(c_inv, *field(got1, 4, 2))
     scale = OMEGA * ci
     a_right, a_left = scale * cr, scale * roll(cr, 1, 1)
     a_down, a_up = scale * cd, scale * roll(cd, 1, 0)
@@ -292,15 +284,13 @@
         return total([a[k] * b[k] for k in range(16)])
 
     sums = {}
-    got = field(g1h, g1v, 3)
-    source, sides, ends = [resid], None, None
+    news = field(got1, 4, 3)
     images, fields = [], []
     for j in range(3):
         if j:
-            for copy in copies:
-                copy.wait()
-            got = field(gh.at[j - 1], gv.at[j - 1])
-        level, new_side, new_ends = smooth(coarse, *got)
+            finish(got.at[j - 1], gx_sem.at[j])
+            news = field(got.at[j - 1], 1, 0)
+        level, new_side, new_ends = smooth(coarse, *news)
         if j == 0:
             v = [inv_ref[k] * resid[k] + level for k in range(16)]
             side, ends = new_side, new_ends
@@ -321,7 +311,7 @@
         if j < 2:
             coarse = total(image)
             pack(coarse, image, sh.at[j], su.at[j], sd.at[j])
-            copies = exchange(sh.at[j], su.at[j], sd.at[j], gh.at[j], gv.at[j], sx_sem.at[j + 1], gx_sem.at[j + 1])
+            exchange(sh.at[j], su.at[j], sd.at[j], got.at[j], 1, sx_sem.at[j + 1], gx_sem.at[j + 1])
         sums["g", j] = dot(resid, v)
         for i in range(j + 1):
             sums[i, j] = dot(images[i], v)
@@ -342,15 +332,12 @@
         (slots_a, na, me_a, partner_a), (slots_b, nb, y, partner_b), (slots_c, nc, z, partner_c)
     ):
         part[base] = sums_row
-        copies = []
         for k in range(1, count):
-            copies.append(pltpu.make_async_remote_copy(
-                part.at[base], slots.at[k], sr_sem.at[base, k], gr_sem.at[base, k],
-                device_id=partner(k), device_id_type=MESH,
-            ))
-            copies[-1].start()
-        for copy in copies:
-            copy.wait()
+            pltpu.make_async_remote_copy(
+                part.at[base], slots.at[k], sr_sem.at[base], gr_sem.at[base], device_id=partner(k), device_id_type=MESH
+            ).start()
+        if count > 1:
+            finish(slots.at[pl.ds(1, count - 1)], gr_sem.at[base])
         sums_row = total_any([sums_row] + [slots[k] for k in range(1, count)])
         base += 1
 
@@ -370,9 +357,21 @@
     c2 = y2 / d2
     c1 = y1 / d1 - l21 * c2
     c0 = g0 / a00 - l10 * c1 - l20 * c2
-    c = [jnp.broadcast_to(v, shape) for v in (c0, c1, c2)]
-
-    stores = []
+    for k, value in enumerate((c0, c1, c2)):
+        c_ref[k] = jnp.broadcast_to(value, (8, 128))
+
+    finish(sent0, s0_sem)
+    finish(got1, sx_sem.at[0])
+    for j in range(2):
+        finish(got.at[j], sx_sem.at[j + 1])
+    for k, slots in enumerate((slots_a, slots_b, slots_c)):
+        if slots.shape[0] > 1:
+            finish(slots.at[pl.ds(1, slots.shape[0] - 1)], sr_sem.at[k])
+
+
+def combine(r0_ref, u_ref, w_ref, c_ref, heights_ref, resid_ref, done, sem):
+    lane = iota((24, 128), 1)
+    c = [jnp.concatenate([c_ref[k]] * 3, axis=0) for k in range(3)]
     for n, out_ref in enumerate((heights_ref, resid_ref)):
         for t in range(4):
             planes = []
@@ -384,12 +383,9 @@
             for v, value in enumerate(undeal(planes, lane)):
                 done[n, v, pl.ds(t, 24, stride=4), :] = value
         for v in range(4):
-            stores.append(
-                pltpu.make_async_copy(done.at[n, v], out_ref.at[:, 128 * v:128 * v + 128], out_sem.at[n, v])
-            )
-            stores[-1].start()
-    for copy in stores:
-        copy.wait()
+            pltpu.make_async_copy(done.at[n, v], out_ref.at[:, 128 * v:128 * v + 128], sem.at[n]).start()
+    for n in range(2):
+        pltpu.make_async_copy(done.at[n], done.at[n], sem.at[n]).wait()
 
 
 def total_any(values):
@@ -405,33 +401,40 @@
     def step(*args):
         rows, cols = args[0].shape
         assert (rows, cols) == (96, 512)
-        tile, planes = pltpu.VMEM((24, 128), F), pltpu.VMEM((16, 24, 128), F)
+        shapes = [(16, 24, 128), (3, 16, 24, 128), (3, 16, 24, 128), (3, 8, 128)]
         dma = pltpu.SemaphoreType.DMA
-        most = max(na, nb, nc)
-        out = pl.pallas_call(
+
+        def vmem(*shape):
+            return pltpu.VMEM(shape, F)
+
+        args = [pltpu.with_memory_space_constraint(x, pltpu.HBM) for x in args]
+        parts = pl.pallas_call(
             functools.partial(kernel, split),
+            out_shape=[jax.ShapeDtypeStruct(shape, F) for shape in shapes],
+            in_specs=[pl.BlockSpec(memory_space=pltpu.HBM)] * 6,
+            out_specs=[pl.BlockSpec(memory_space=pltpu.VMEM)] * 4,
+            scratch_shapes=[
+                vmem(6, 4, rows, 128),
+                vmem(16, 24, 128), vmem(16, 24, 128), vmem(16, 24, 128), vmem(16, 24, 128),
+                vmem(4, 24, 128), vmem(4, 24, 128),
+                vmem(4, 8, 128), vmem(4, 8, 128),
+                vmem(12, 8, 128), vmem(4, 8, 128), vmem(4, 8, 128), vmem(48, 8, 128),
+                vmem(2, 3, 8, 128), vmem(2, 1, 8, 128), vmem(2, 1, 8, 128), vmem(2, 12, 8, 128),
+                vmem(3, 1, 128), vmem(na, 1, 128), vmem(nb, 1, 128), vmem(nc, 1, 128),
+                dma((6,)), dma(()), dma(()), dma((3,)), dma((3,)), dma((3,)), dma((3,)),
+            ],
+            compiler_params=pltpu.CompilerParams(
+                collective_id=0, has_side_effects=True, vmem_limit_bytes=12 * 2**20
+            ),
+        )(*args)
+        return tuple(pl.pallas_call(
+            combine,
             out_shape=[jax.ShapeDtypeStruct((rows, cols), F)] * 2,
-            in_specs=[pl.BlockSpec(memory_space=pltpu.HBM)] * 6,
+            in_specs=[pl.BlockSpec(memory_space=pltpu.VMEM)] * 4,
             out_specs=[pl.BlockSpec(memory_space=pltpu.HBM)] * 2,
-            scratch_shapes=[
-                pltpu.VMEM((6, 4, rows, 128), F),
-                planes, planes, planes, planes,
-                pltpu.VMEM((4, 24, 128), F), pltpu.VMEM((4, 24, 128), F),
-                planes,
-                pltpu.VMEM((3, 16, 24, 128), F), pltpu.VMEM((3, 16, 24, 128), F),
-                tile, pltpu.VMEM((8, 128), F), tile, pltpu.VMEM((8, 128), F),
-                pltpu.VMEM((4, 24, 128), F), pltpu.VMEM((4, 8, 128), F), pltpu.VMEM((4, 8, 128), F),
-                pltpu.VMEM((2, 4, 24, 128), F), pltpu.VMEM((6, 4, 8, 128), F),
-                pltpu.VMEM((2, 24, 128), F), pltpu.VMEM((2, 8, 128), F), pltpu.VMEM((2, 8, 128), F),
-                pltpu.VMEM((2, 2, 24, 128), F), pltpu.VMEM((2, 6, 8, 128), F),
-                pltpu.VMEM((3, 1, 128), F),
-                pltpu.VMEM((na, 1, 128), F), pltpu.VMEM((nb, 1, 128), F), pltpu.VMEM((nc, 1, 128), F),
-                pltpu.VMEM((2, 4, rows, 128), F),
-                dma((6, 4)), dma((2, 4)), dma((2,)), dma((2,)), dma((3, 8)), dma((3, 8)), dma((3, most)), dma((3, most)),
-            ],
-            compiler_params=pltpu.CompilerParams(collective_id=0, has_side_effects=True),
-        )(*args)
-        return tuple(out)
+            scratch_shapes=[vmem(2, 4, rows, 128), dma((2,))],
+            compiler_params=pltpu.CompilerParams(vmem_limit_bytes=12 * 2**20),
+        )(*parts))
 
     return jax.shard_map(
         step,

time: 52.5 us -> 49 us (0.933)
  local copies, waits for them, and re-layouts: 2.34 us -> 0 us
  Pallas kernels: 49 us -> 47.9 us
    unnamed x4 -> x0, local copies, waits for them, and re-layouts: 2.34 us -> none
    pallas_call x1, Pallas kernels: 49 us -> 46.9 us  [step(): pl.pallas_call(functools.partial(kernel, split), out_shape=[jax.ShapeDtyp...]
    pallas_call x0 -> x1, Pallas kernels: none -> 0.96 us  [step(): pl.pallas_call(combine, out_shape=[jax.ShapeDtypeStruct((rows, cols), F)]...]
where the time goes in v2:
time: 49 us; the launch traced here: 48.5 us
  Pallas kernels  47.9 us (98%)
  between operations  0.64 us (1%)
    pallas_call x1, Pallas kernels, step(): pl.pallas_call(functools.partial(kernel, split), out_shape=[jax.ShapeDtyp...  46.9 us

profile of v2, /device:TPU:1, one launch (start us, length us, event | category | flops | bytes accessed | tf_op | source)
XLA Modules:
  0.0 48.5 jit_solution(17592046378610508136)
XLA Ops:
  0.6 46.9 %shard_map.77 = (f32[16,24,128]{2,1,0:T(8,128)S(1)}, f32[3,16,24,128]{3,2,1,0:T(8,128)S(1)}, f32[3,16,24,128]{3,2,1,0:T(8,128)S(1)}, f32[3,8,128]{2,1,0:T(8,128)S(1)}) custom-call(f32[96,512]{1,0:T(8,128)} %refs_0_.1, f32[96,512]{1,0:T(8,128)} %refs_1_.1, f32[96,512]{1,0:T(8,128)} %refs_2_.1, f32[96,512]{1,0:T(8,128)} %refs_3_.1, f32[96,512]{1,0:T(8,128)} %refs_4_.1, ...), custom_call_target="tpu_custom_call" | custom-call | tf_op jit(solution)/shard_map/pallas_call | solution.py:411
  47.6 1.0 %shard_map.78 = (f32[96,512]{1,0:T(8,128)}, f32[96,512]{1,0:T(8,128)}) custom-call(f32[16,24,128]{2,1,0:T(8,128)S(1)} %get-tuple-element.6.r0_ref, f32[3,16,24,128]{3,2,1,0:T(8,128)S(1)} %get-tuple-element.7.u_ref, f32[3,16,24,128]{3,2,1,0:T(8,128)S(1)} %get-tuple-element.8.w_ref, f32[3,8,128]{2,1,0:T(8,128)S(1)} %get-tuple-element.9.c_ref), custom_call_target="tpu_custom_call" | custom-call | tf_op jit(solution)/shard_map/pallas_call | solution.py:430

commit v3 on v2

--- a/solution.py
+++ b/solution.py
@@ -60,9 +60,9 @@
     inputs, refs = refs[:6], refs[6:]
     r0_ref, u_ref, w_ref, c_ref = refs[:4]
     (raw, rw_ref, dw_ref, diag_ref, inv_ref, lw_ref, uw_ref,
-     sent0, got0, s1h, s1u, s1d, got1, sh, su, sd, got,
+     s1h, s1u, s1d, got1, sh, su, sd, got,
      part, slots_a, slots_b, slots_c,
-     in_sem, s0_sem, g0_sem, sx_sem, gx_sem, sr_sem, gr_sem) = refs[4:]
+     in_sem, sx_sem, gx_sem, sr_sem, gr_sem) = refs[4:]
 
     row, col = lax.axis_index("row"), lax.axis_index("col")
     up, down = lax.rem(row + nrow - 1, nrow), lax.rem(row + 1, nrow)
@@ -141,42 +141,166 @@
         dw[12 + s] = jnp.where(at_end, 0.0, dw[12 + s])
     fx = [a * b for a, b in zip(rw, load(0))]
     fy = [a * b for a, b in zip(dw, load(1))]
-    sent0[:3] = pack_cols(fx[3::4], 127, 124, pack_cols(rw[3::4], 127, 120)).reshape(3, 8, 128)
-    sent0[3] = pack_rows(fy[12:], 23, 4, pack_rows(dw[12:], 23, 0))
+    anchor = load(4)
+    prior = load(5)
+
+    def behind(planes):
+        return [jnp.where(lane == 0, 0.0, roll(planes[4 * t + 3], 1, 1)) for t in range(4)]
+
+    def above(planes):
+        return [jnp.where(sub == 0, 0.0, roll(planes[12 + s], 1, 0)) for s in range(4)]
+
+    def spread(first, planes, step):
+        if step == 1:
+            return [first[k // 4] if k % 4 == 0 else planes[k - 1] for k in range(16)]
+        return [first[k] if k < 4 else planes[k - 4] for k in range(16)]
+
+    lw0, fl0, uw0, fu0 = behind(rw), behind(fx), above(dw), above(fy)
+    lw, fl, uw, fu = spread(lw0, rw, 1), spread(fl0, fx, 1), spread(uw0, dw, 4), spread(fu0, fy, 4)
+    diag = [anchor[k] + lw[k] + rw[k] + uw[k] + dw[k] for k in range(16)]
+    resid = [anchor[k] * prior[k] - fx[k] - fy[k] + fl[k] + fu[k] for k in range(16)]
+
+    def total(planes):
+        while len(planes) > 1:
+            planes = [a + b for a, b in zip(planes[::2], planes[1::2])]
+        return planes[0]
+
+    c_right, c_down = total(rw[3::4]), total(dw[12:])
+    c_diag = total(anchor) + total(lw0) + c_right + total(uw0) + c_down
+    c_resid, c_fx, c_fy = total(resid), total(fx[3::4]), total(fy[12:])
+
+    def side_tile(coarse, planes=None, edge=None):
+        h = coarse
+        if planes is not None:
+            h = pack_cols(planes[3::4], 127, 120, pack_cols(planes[0::4], 0, 4, h))
+        if edge is not None:
+            h = pack_cols(edge[3::4], 127, 116, h)
+        return h
+
+    h0, h1 = side_tile(c_right, diag, rw), side_tile(c_down, resid, fx)
+    h2 = jnp.where(lane == 119, roll(c_fx, -8, 1), c_diag)
+    h3 = jnp.where(
+        jnp.logical_and(lane >= 4, lane < 8), roll(c_fy, 4, 1),
+        jnp.where(jnp.logical_and(lane >= 120, lane < 124), roll(c_fy, -4, 1), c_resid),
+    )
+    for k, h in enumerate((h0, h1, h2, h3)):
+        s1h[3 * k:3 * k + 3] = h.reshape(3, 8, 128)
+    s1u[0] = pack_rows(diag[:4], 0, 4, c_right[:8])
+    s1u[1] = pack_rows(resid[:4], 0, 4, c_down[:8])
+    s1u[2] = jnp.where(sub8 < 4, c_diag[:8], roll(c_fx[:8], 4, 0))
+    s1u[3] = pack_rows([rw[3], fx[3]], 0, 4, c_resid[:8])
+    s1d[0] = pack_rows(diag[12:], 23, 0, c_right[16:])
+    s1d[1] = pack_rows(resid[12:], 23, 0, c_down[16:])
+    s1d[2] = jnp.where(sub8 >= 4, c_diag[16:], roll(c_fx[16:], 4, 0))
+    s1d[3] = pack_rows([c_fy, rw[15], fx[15]], 23, 0, c_resid[16:])
+    d4 = pack_rows(fy[12:], 23, 4, pack_rows(dw[12:], 23, 0))
+    s1d[4] = d4
+
+    def pack(coarse, planes, h_ref, u_ref, d_ref):
+        h_ref[...] = side_tile(coarse, planes).reshape(3, 8, 128)
+        u_ref[0] = pack_rows(planes[:4], 0, 4, coarse[:8])
+        d_ref[0] = pack_rows(planes[12:], 23, 0, coarse[16:])
+
+    def exchange(h, u, d, got, nu, nd, send, recv):
+        nh = h.shape[0]
+        plan = [(u, 1, (up, left)), (u, 2, (up, right)), (d, 4, (down, left)), (d, 5, (down, right))]
+        plan += [(u, 0, (up, col)), (d, 3, (down, col))]
+        plan = [
+            (src, got.at[pl.ds(2 * nh + (nu * k if k < 3 else 3 * nu + nd * (k - 3)), nu if k < 3 else nd)], who)
+            for src, k, who in plan
+        ]
+        plan += [(h, got.at[pl.ds(0, nh)], (row, left)), (h, got.at[pl.ds(nh, nh)], (row, right))]
+        for src, dst, who in plan:
+            pltpu.make_async_remote_copy(src, dst, send, recv, device_id=who, device_id_type=MESH).start()
+
     pl.semaphore_wait(barrier, len(partners))
-    for part0, who in ((pl.ds(0, 3), (row, right)), (pl.ds(3, 1), (down, col))):
-        pltpu.make_async_remote_copy(
-            sent0.at[part0], got0.at[part0], s0_sem, g0_sem, device_id=who, device_id_type=MESH
-        ).start()
+    exchange(s1h, s1u, s1d, got1, 4, 5, sx_sem.at[0], gx_sem.at[0])
     for k in range(16):
         rw_ref[k] = rw[k]
         dw_ref[k] = dw[k]
-    anchor = load(4)
-    prior = load(5)
-    source = [anchor[k] * prior[k] - fx[k] - fy[k] for k in range(16)]
-    finish(got0, g0_sem)
-
-    def shift_left_edge(planes, halo, base):
-        return [jnp.where(lane == 0, roll(halo, -(base + t), 1), roll(planes[t], 1, 1)) for t in range(4)]
-
-    def shift_up_edge(planes, halo, base):
-        return [
-            jnp.where(sub == 0, jnp.broadcast_to(halo[base + s:base + s + 1], shape), roll(planes[s], 1, 0))
-            for s in range(4)
-        ]
-
-    halo = got0[:3].reshape(shape)
-    lw0 = shift_left_edge(rw[3::4], halo, 120)
-    fl0 = shift_left_edge(fx[3::4], halo, 124)
-    halo = got0[3]
-    uw0 = shift_up_edge(dw[12:], halo, 0)
-    fu0 = shift_up_edge(fy[12:], halo, 4)
-    lw = [lw0[k // 4] if k % 4 == 0 else rw[k - 1] for k in range(16)]
-    fl = [fl0[k // 4] if k % 4 == 0 else fx[k - 1] for k in range(16)]
-    uw = [uw0[k] if k < 4 else dw[k - 4] for k in range(16)]
-    fu = [fu0[k] if k < 4 else fy[k - 4] for k in range(16)]
-    diag = [anchor[k] + lw[k] + rw[k] + uw[k] + dw[k] for k in range(16)]
-    resid = [source[k] + fl[k] + fu[k] for k in range(16)]
+
+    def assemble(own, h, v, fill=0.0):
+        side = jnp.where(lane < 64, h[0], h[1])
+        ring = jnp.where(jnp.logical_or(lane < 4, lane >= 124), side, fill)
+        below = jnp.where(sub8 < 4, v[0], v[3])
+        corner = jnp.where(
+            lane8 < 4,
+            jnp.where(sub8 < 4, v[1], v[4]),
+            jnp.where(lane8 >= 124, jnp.where(sub8 < 4, v[2], v[5]), fill),
+        )
+        ends = jnp.where(sub8 < 4, v[3], v[0])
+        return quad(own, ring, below, corner), side, ends
+
+    def quad(own, ring, below, corner):
+        return jnp.concatenate(
+            [jnp.concatenate([own, ring], axis=1), jnp.concatenate([below, corner], axis=1)], axis=0
+        )
+
+    finish(got1, gx_sem.at[0])
+    hs = [[got1[pl.ds(12 * k + 3 * f, 3)].reshape(shape) for k in range(2)] for f in range(4)]
+    vs = [[got1[24 + 4 * k + f] for k in range(3)] + [got1[36 + 5 * k + f] for k in range(3)] for f in range(4)]
+    from_up, from_up_right, from_up_left = (got1[36 + 5 * k + 4] for k in range(3))
+
+    cr, diag_side, diag_ends = assemble(c_right, hs[0], vs[0])
+    cd, side, ends = assemble(c_down, hs[1], vs[1])
+    cdiag, _, _ = assemble(c_diag, hs[2], vs[2], 1.0)
+    ext, _, _ = assemble(c_resid, hs[3], vs[3])
+
+    lane_x, sub_x = iota((32, 256), 1), iota((32, 256), 0)
+    first_col = (lane_x & 127) == 0
+    first_row = jnp.logical_or(sub_x == 0, sub_x == 24)
+    cdiag = cdiag + jnp.where(first_col, roll(cr, 1, 1), 0.0) + jnp.where(first_row, roll(cd, 1, 0), 0.0)
+    across = quad(
+        roll(hs[2][1], 9, 1),
+        roll(c_fx, 1, 1),
+        roll(roll(jnp.where(sub8 < 4, vs[2][5], vs[2][2]), 4, 0), 1, 1),
+        roll(roll(jnp.where(sub8 < 4, vs[2][3], vs[2][0]), 4, 0), 1, 1),
+    )
+    ext = ext + jnp.where(first_col, across, 0.0)
+    beyond = jnp.where(lane8 < 64, vs[3][4], vs[3][5])
+    near = jnp.where(lane < 64, roll(hs[3][0], -4, 1), roll(hs[3][1], 4, 1))
+    across = quad(
+        jnp.broadcast_to(vs[3][3][0:1], shape),
+        jnp.broadcast_to(beyond[0:1], shape),
+        roll(c_fy[16:], 1, 0),
+        roll(near[16:], 1, 0),
+    )
+    in_ring = jnp.logical_or(lane_x < 132, lane_x >= 252)
+    ext = ext + jnp.where(jnp.logical_and(first_row, in_ring), across, 0.0)
+
+    to_right = jnp.logical_and(lane >= 4, lane < 8)
+    to_left = jnp.logical_and(lane >= 120, lane < 124)
+    top_right = jnp.logical_and(sub == 0, lane == 4)
+    top_left = jnp.logical_and(sub == 0, lane == 120)
+    far_right, far_left = roll(from_up_right, 4, 1), roll(from_up_left, -7, 1)
+    col_up, col_down = roll(vs[3][5], 1, 1), roll(vs[3][2], 1, 1)
+    up_corner = jnp.logical_and(lane8 == 0, sub8 == 0)
+    down_corner = jnp.logical_and(lane8 == 0, sub8 == 4)
+
+    def complete(at_side, at_ends, edge, row_edge, n):
+        at_side = at_side + jnp.where(to_right, roll(edge, 16, 1), 0.0)
+        at_side = at_side + jnp.where(top_right, jnp.broadcast_to(far_right[4 * n:4 * n + 1], shape), 0.0)
+        at_side = at_side + jnp.where(top_left, jnp.broadcast_to(far_left[4 * n + 3:4 * n + 4], shape), 0.0)
+        at_ends = at_ends + jnp.where(sub8 >= 4, row_edge, 0.0)
+        at_ends = at_ends + jnp.where(up_corner, jnp.broadcast_to(col_up[1 + n:2 + n], (8, 128)), 0.0)
+        at_ends = at_ends + jnp.where(down_corner, jnp.broadcast_to(col_down[4 + n:5 + n], (8, 128)), 0.0)
+        return at_side, at_ends
+
+    diag_side, diag_ends = complete(diag_side, diag_ends, h0, roll(d4, 4, 0), 0)
+    side, ends = complete(side, ends, h1, d4, 1)
+    inv_side = 1.0 / jnp.where(jnp.logical_or(to_right, to_left), diag_side, 1.0)
+    inv_ends = 1.0 / diag_ends
+
+    for t in range(4):
+        more = jnp.where(lane == 0, roll(hs[0][1], -(116 + t), 1), 0.0)
+        lw0[t] = lw0[t] + more
+        diag[4 * t] = diag[4 * t] + more
+        resid[4 * t] = resid[4 * t] + jnp.where(lane == 0, roll(hs[1][1], -(116 + t), 1), 0.0)
+    for s in range(4):
+        more = jnp.where(sub == 0, jnp.broadcast_to(from_up[s:s + 1], shape), 0.0)
+        uw0[s] = uw0[s] + more
+        diag[s] = diag[s] + more
+        resid[s] = resid[s] + jnp.where(sub == 0, jnp.broadcast_to(from_up[4 + s:5 + s], shape), 0.0)
     inv = [1.0 / d for d in diag]
     for k in range(16):
         diag_ref[k] = diag[k]
@@ -186,68 +310,11 @@
         lw_ref[k] = lw0[k]
         uw_ref[k] = uw0[k]
 
-    def total(planes):
-        while len(planes) > 1:
-            planes = [a + b for a, b in zip(planes[::2], planes[1::2])]
-        return planes[0]
-
-    c_right, c_down = total(rw[3::4]), total(dw[12:])
-    c_inv = 1.0 / (total(anchor) + total(lw0) + c_right + total(uw0) + c_down)
-
-    def pack(coarse, planes, h_ref, u_ref, d_ref):
-        h, u, d = coarse, coarse[:8], coarse[16:]
-        if planes is not None:
-            h = pack_cols(planes[3::4], 127, 120, pack_cols(planes[0::4], 0, 4, h))
-            u = pack_rows(planes[:4], 0, 4, u)
-            d = pack_rows(planes[12:], 23, 0, d)
-        h_ref[...] = h.reshape(3, 8, 128)
-        u_ref[0] = u
-        d_ref[0] = d
-
-    def exchange(h, u, d, got, n, send, recv):
-        plan = [(u, 1, (up, left)), (u, 2, (up, right)), (d, 4, (down, left)), (d, 5, (down, right))]
-        plan += [(u, 0, (up, col)), (d, 3, (down, col))]
-        plan = [(src, got.at[pl.ds((6 + slot) * n, n)], who) for src, slot, who in plan]
-        plan += [(h, got.at[pl.ds(0, 3 * n)], (row, left)), (h, got.at[pl.ds(3 * n, 3 * n)], (row, right))]
-        for src, dst, who in plan:
-            pltpu.make_async_remote_copy(src, dst, send, recv, device_id=who, device_id_type=MESH).start()
-
-    coarse = total(resid)
-    pack(c_right, inv, s1h.at[pl.ds(0, 3)], s1u.at[pl.ds(0, 1)], s1d.at[pl.ds(0, 1)])
-    pack(c_down, None, s1h.at[pl.ds(3, 3)], s1u.at[pl.ds(1, 1)], s1d.at[pl.ds(1, 1)])
-    pack(c_inv, None, s1h.at[pl.ds(6, 3)], s1u.at[pl.ds(2, 1)], s1d.at[pl.ds(2, 1)])
-    pack(coarse, resid, s1h.at[pl.ds(9, 3)], s1u.at[pl.ds(3, 1)], s1d.at[pl.ds(3, 1)])
-    exchange(s1h, s1u, s1d, got1, 4, sx_sem.at[0], gx_sem.at[0])
-
-    def assemble(own, h, v):
-        side = jnp.where(lane < 64, h[0], h[1])
-        ring = jnp.where(jnp.logical_or(lane < 4, lane >= 124), side, 0.0)
-        below = jnp.where(sub8 < 4, v[0], v[3])
-        corner = jnp.where(
-            lane8 < 4,
-            jnp.where(sub8 < 4, v[1], v[4]),
-            jnp.where(lane8 >= 124, jnp.where(sub8 < 4, v[2], v[5]), 0.0),
-        )
-        ends = jnp.where(sub8 < 4, v[3], v[0])
-        ext = jnp.concatenate(
-            [jnp.concatenate([own, ring], axis=1), jnp.concatenate([below, corner], axis=1)], axis=0
-        )
-        return ext, side, ends
-
-    def field(ref, n, f):
-        h = [ref[pl.ds(3 * (n * k + f), 3)].reshape(shape) for k in range(2)]
-        return h, [ref[n * (6 + k) + f] for k in range(6)]
-
-    finish(got1, gx_sem.at[0])
-    cr, inv_side, inv_ends = assemble(c_right, *field(got1, 4, 0))
-    cd, _, _ = assemble(c_down, *field(got1, 4, 1))
-    ci, _, _ = assemble(c_inv, *field(got1, 4, 2))
-    scale = OMEGA * ci
+    scale = OMEGA / cdiag
     a_right, a_left = scale * cr, scale * roll(cr, 1, 1)
     a_down, a_up = scale * cd, scale * roll(cd, 1, 0)
 
-    def smooth(own, h, v):
-        ext, side, ends = assemble(own, h, v)
+    def smooth(ext, side, ends):
         start = scale * ext
         level = start
         for turn in range(3):
@@ -284,13 +351,15 @@
         return total([a[k] * b[k] for k in range(16)])
 
     sums = {}
-    news = field(got1, 4, 3)
+    news = ext, side, ends
     images, fields = [], []
     for j in range(3):
         if j:
             finish(got.at[j - 1], gx_sem.at[j])
-            news = field(got.at[j - 1], 1, 0)
-        level, new_side, new_ends = smooth(coarse, *news)
+            news = assemble(
+                coarse, [got[j - 1, 3 * k:3 * k + 3].reshape(shape) for k in range(2)], [got[j - 1, 6 + k] for k in range(6)]
+            )
+        level, new_side, new_ends = smooth(*news)
         if j == 0:
             v = [inv_ref[k] * resid[k] + level for k in range(16)]
             side, ends = new_side, new_ends
@@ -311,7 +380,7 @@
         if j < 2:
             coarse = total(image)
             pack(coarse, image, sh.at[j], su.at[j], sd.at[j])
-            exchange(sh.at[j], su.at[j], sd.at[j], got.at[j], 1, sx_sem.at[j + 1], gx_sem.at[j + 1])
+            exchange(sh.at[j], su.at[j], sd.at[j], got.at[j], 1, 1, sx_sem.at[j + 1], gx_sem.at[j + 1])
         sums["g", j] = dot(resid, v)
         for i in range(j + 1):
             sums[i, j] = dot(images[i], v)
@@ -360,7 +429,6 @@
     for k, value in enumerate((c0, c1, c2)):
         c_ref[k] = jnp.broadcast_to(value, (8, 128))
 
-    finish(sent0, s0_sem)
     finish(got1, sx_sem.at[0])
     for j in range(2):
         finish(got.at[j], sx_sem.at[j + 1])
@@ -417,11 +485,10 @@
                 vmem(6, 4, rows, 128),
                 vmem(16, 24, 128), vmem(16, 24, 128), vmem(16, 24, 128), vmem(16, 24, 128),
                 vmem(4, 24, 128), vmem(4, 24, 128),
-                vmem(4, 8, 128), vmem(4, 8, 128),
-                vmem(12, 8, 128), vmem(4, 8, 128), vmem(4, 8, 128), vmem(48, 8, 128),
+                vmem(12, 8, 128), vmem(4, 8, 128), vmem(5, 8, 128), vmem(51, 8, 128),
                 vmem(2, 3, 8, 128), vmem(2, 1, 8, 128), vmem(2, 1, 8, 128), vmem(2, 12, 8, 128),
                 vmem(3, 1, 128), vmem(na, 1, 128), vmem(nb, 1, 128), vmem(nc, 1, 128),
-                dma((6,)), dma(()), dma(()), dma((3,)), dma((3,)), dma((3,)), dma((3,)),
+                dma((6,)), dma((3,)), dma((3,)), dma((3,)), dma((3,)),
             ],
             compiler_params=pltpu.CompilerParams(
                 collective_id=0, has_side_effects=True, vmem_limit_bytes=12 * 2**20

time: 49 us -> 46 us (0.939)
  Pallas kernels: 47.9 us -> 44.5 us
    pallas_call x1, Pallas kernels: 46.9 us -> 43.5 us  [step(): pl.pallas_call(functools.partial(kernel, split), out_shape=[jax.ShapeDtyp...]
where the time goes in v3:
time: 46 us; the launch traced here: 45.1 us
  Pallas kernels  44.5 us (97%)
  between operations  0.64 us (1%)
    pallas_call x1, Pallas kernels, step(): pl.pallas_call(functools.partial(kernel, split), out_shape=[jax.ShapeDtyp...  43.5 us
    pallas_call x1, Pallas kernels, step(): pl.pallas_call(combine, out_shape=[jax.ShapeDtypeStruct((rows, cols), F)]...  0.96 us

profile of v3, /device:TPU:1, one launch (start us, length us, event | category | flops | bytes accessed | tf_op | source)
XLA Modules:
  0.0 45.1 jit_solution(8975735171211663499)
XLA Ops:
  0.6 43.5 %shard_map.77 = (f32[16,24,128]{2,1,0:T(8,128)S(1)}, f32[3,16,24,128]{3,2,1,0:T(8,128)S(1)}, f32[3,16,24,128]{3,2,1,0:T(8,128)S(1)}, f32[3,8,128]{2,1,0:T(8,128)S(1)}) custom-call(f32[96,512]{1,0:T(8,128)} %refs_0_.1, f32[96,512]{1,0:T(8,128)} %refs_1_.1, f32[96,512]{1,0:T(8,128)} %refs_2_.1, f32[96,512]{1,0:T(8,128)} %refs_3_.1, f32[96,512]{1,0:T(8,128)} %refs_4_.1, ...), custom_call_target="tpu_custom_call" | custom-call | tf_op jit(solution)/shard_map/pallas_call | solution.py:479
  44.1 1.0 %shard_map.78 = (f32[96,512]{1,0:T(8,128)}, f32[96,512]{1,0:T(8,128)}) custom-call(f32[16,24,128]{2,1,0:T(8,128)S(1)} %get-tuple-element.6.r0_ref, f32[3,16,24,128]{3,2,1,0:T(8,128)S(1)} %get-tuple-element.7.u_ref, f32[3,16,24,128]{3,2,1,0:T(8,128)S(1)} %get-tuple-element.8.w_ref, f32[3,8,128]{2,1,0:T(8,128)S(1)} %get-tuple-element.9.c_ref), custom_call_target="tpu_custom_call" | custom-call | tf_op jit(solution)/shard_map/pallas_call | solution.py:497

commit v4 on v3

--- a/solution.py
+++ b/solution.py
@@ -58,16 +58,18 @@
     ny, nzh, ncore, nzl, nx = (split[k] for k in ("y", "zh", "core", "zl", "x"))
     nrow, ncol = ny * nzh * ncore, nzl * nx
     inputs, refs = refs[:6], refs[6:]
-    r0_ref, u_ref, w_ref, c_ref = refs[:4]
+    kept_ref, c_ref = refs[:2]
     (raw, rw_ref, dw_ref, diag_ref, inv_ref, lw_ref, uw_ref,
-     s1h, s1u, s1d, got1, sh, su, sd, got,
-     part, slots_a, slots_b, slots_c,
-     in_sem, sx_sem, gx_sem, sr_sem, gr_sem) = refs[4:]
-
+     s1h, s1u, s1d, sh, su, sd, landed,
+     part, slots,
+     in_sem, sx_sem, gx_sem, sr_sem, gr_sem) = refs[2:]
+
+    got1 = landed.at[pl.ds(0, 51)]
+    got = [landed.at[pl.ds(51 + 12 * j, 12)] for j in range(2)]
     row, col = lax.axis_index("row"), lax.axis_index("col")
     up, down = lax.rem(row + nrow - 1, nrow), lax.rem(row + 1, nrow)
     left, right = lax.rem(col + ncol - 1, ncol), lax.rem(col + 1, ncol)
-    neighbours = [(up, col), (up, left), (up, right), (down, col), (down, left), (down, right), (row, left), (row, right)]
+    neighbours = [(up, left), (up, right), (down, left), (down, right), (up, col), (down, col), (row, left), (row, right)]
 
     y, zh, core = row // (nzh * ncore), lax.rem(row // ncore, nzh), lax.rem(row, ncore)
     zl, x = col // nx, lax.rem(col, nx)
@@ -76,18 +78,22 @@
     def device(y, z, core, x):
         return ((y * nzh + z // nzl) * ncore + core, lax.rem(z, nzl) * nx + x)
 
-    na, nb, nc = nx * ncore, ny, nzh * nzl
-    me_a = x * ncore + core
-
-    def partner_a(k):
-        other = lax.rem(me_a + k, na)
-        return device(y, z, lax.rem(other, ncore), other // ncore)
-
-    def partner_b(k):
-        return device(lax.rem(y + k, ny), z, core, x)
-
-    def partner_c(k):
-        return device(y, lax.rem(z + k, nc), core, x)
+    nz = nzh * nzl
+
+    def ring(k, n):
+        return min(k, n - k)
+
+    stage_a = sorted(((ring(i, nx) + ring(k, nz), i, k) for i in range(nx) for k in range(nz) if i or k), reverse=True)
+    stage_b = sorted(((ring(k, ny), k, i) for k in range(ny) for i in range(ncore) if i or k), reverse=True)
+    hops_a = [far for far, _, _ in stage_a]
+    stage_a = [device(y, lax.rem(z + k, nz), core, lax.rem(x + i, nx)) for _, i, k in stage_a]
+    stage_b = [device(lax.rem(y + k, ny), z, lax.rem(core + i, ncore), x) for _, k, i in stage_b]
+
+    farther = sum(far > 5 for far in hops_a)
+    partners = stage_a[:farther] + neighbours + stage_a[farther:] + stage_b
+    barrier = pltpu.get_barrier_semaphore()
+    for who in partners[:farther + 8]:
+        pl.semaphore_signal(barrier, inc=1, device_id=who, device_id_type=MESH)
 
     loads = [
         [pltpu.make_async_copy(src.at[:, 128 * v:128 * v + 128], raw.at[k, v], in_sem.at[k]) for v in range(4)]
@@ -97,10 +103,7 @@
         for copy in loads[k]:
             copy.start()
 
-    partners = neighbours + [partner_a(k) for k in range(1, na)]
-    partners += [partner_b(k) for k in range(1, nb)] + [partner_c(k) for k in range(1, nc)]
-    barrier = pltpu.get_barrier_semaphore()
-    for who in partners:
+    for who in partners[farther + 8:]:
         pl.semaphore_signal(barrier, inc=1, device_id=who, device_id_type=MESH)
 
     def finish(ref, sem):
@@ -214,7 +217,7 @@
             pltpu.make_async_remote_copy(src, dst, send, recv, device_id=who, device_id_type=MESH).start()
 
     pl.semaphore_wait(barrier, len(partners))
-    exchange(s1h, s1u, s1d, got1, 4, 5, sx_sem.at[0], gx_sem.at[0])
+    exchange(s1h, s1u, s1d, got1, 4, 5, sx_sem, gx_sem.at[0])
     for k in range(16):
         rw_ref[k] = rw[k]
         dw_ref[k] = dw[k]
@@ -305,7 +308,6 @@
     for k in range(16):
         diag_ref[k] = diag[k]
         inv_ref[k] = inv[k]
-        r0_ref[k] = resid[k]
     for k in range(4):
         lw_ref[k] = lw0[k]
         uw_ref[k] = uw0[k]
@@ -355,9 +357,9 @@
     images, fields = [], []
     for j in range(3):
         if j:
-            finish(got.at[j - 1], gx_sem.at[j])
+            finish(got[j - 1], gx_sem.at[j])
             news = assemble(
-                coarse, [got[j - 1, 3 * k:3 * k + 3].reshape(shape) for k in range(2)], [got[j - 1, 6 + k] for k in range(6)]
+                coarse, [got[j - 1][3 * k:3 * k + 3].reshape(shape) for k in range(2)], [got[j - 1][6 + k] for k in range(6)]
             )
         level, new_side, new_ends = smooth(*news)
         if j == 0:
@@ -372,15 +374,12 @@
             image[k] = value
 
         operate(v, side, ends, emit)
-        for k in range(16):
-            u_ref[j, k] = v[k]
-            w_ref[j, k] = image[k]
         fields.append(v)
         images.append(image)
         if j < 2:
             coarse = total(image)
             pack(coarse, image, sh.at[j], su.at[j], sd.at[j])
-            exchange(sh.at[j], su.at[j], sd.at[j], got.at[j], 1, 1, sx_sem.at[j + 1], gx_sem.at[j + 1])
+            exchange(sh.at[j], su.at[j], sd.at[j], got[j], 1, 1, sx_sem, gx_sem.at[j + 1])
         sums["g", j] = dot(resid, v)
         for i in range(j + 1):
             sums[i, j] = dot(images[i], v)
@@ -396,19 +395,23 @@
         one = jnp.sum(x8, axis=0, keepdims=True)
         sums_row = jnp.where((lane1 >> 3) == k, one, sums_row)
 
+    def keep(n, planes):
+        for t in range(4):
+            for v, value in enumerate(undeal(planes[4 * t:4 * t + 4], lane)):
+                kept_ref[n, v, pl.ds(t, 24, stride=4), :] = value
+
     base = 0
-    for slots, count, me, partner in (
-        (slots_a, na, me_a, partner_a), (slots_b, nb, y, partner_b), (slots_c, nc, z, partner_c)
-    ):
-        part[base] = sums_row
-        for k in range(1, count):
+    for stage, others in enumerate((stage_a, stage_b)):
+        part[stage] = sums_row
+        for k, who in enumerate(others):
             pltpu.make_async_remote_copy(
-                part.at[base], slots.at[k], sr_sem.at[base], gr_sem.at[base], device_id=partner(k), device_id_type=MESH
+                part.at[stage], slots.at[base + k], sr_sem, gr_sem.at[stage], device_id=who, device_id_type=MESH
             ).start()
-        if count > 1:
-            finish(slots.at[pl.ds(1, count - 1)], gr_sem.at[base])
-        sums_row = total_any([sums_row] + [slots[k] for k in range(1, count)])
-        base += 1
+        for n in range(4) if stage == 0 else range(4, 7):
+            keep(n, resid if n == 0 else (fields[n - 1] if n < 4 else images[n - 4]))
+        finish(slots.at[pl.ds(base, len(others))], gr_sem.at[stage])
+        sums_row = total_any([sums_row] + [slots[base + k] for k in range(len(others))])
+        base += len(others)
 
     for shift in (4, 2, 1):
         sums_row = sums_row + roll(sums_row, -shift, 1)
@@ -429,31 +432,20 @@
     for k, value in enumerate((c0, c1, c2)):
         c_ref[k] = jnp.broadcast_to(value, (8, 128))
 
-    finish(got1, sx_sem.at[0])
-    for j in range(2):
-        finish(got.at[j], sx_sem.at[j + 1])
-    for k, slots in enumerate((slots_a, slots_b, slots_c)):
-        if slots.shape[0] > 1:
-            finish(slots.at[pl.ds(1, slots.shape[0] - 1)], sr_sem.at[k])
-
-
-def combine(r0_ref, u_ref, w_ref, c_ref, heights_ref, resid_ref, done, sem):
-    lane = iota((24, 128), 1)
-    c = [jnp.concatenate([c_ref[k]] * 3, axis=0) for k in range(3)]
-    for n, out_ref in enumerate((heights_ref, resid_ref)):
-        for t in range(4):
-            planes = []
-            for k in range(4 * t, 4 * t + 4):
-                if n == 0:
-                    planes.append(c[0] * u_ref[0, k] + c[1] * u_ref[1, k] + c[2] * u_ref[2, k])
-                else:
-                    planes.append(r0_ref[k] - (c[0] * w_ref[0, k] + c[1] * w_ref[1, k] + c[2] * w_ref[2, k]))
-            for v, value in enumerate(undeal(planes, lane)):
-                done[n, v, pl.ds(t, 24, stride=4), :] = value
-        for v in range(4):
-            pltpu.make_async_copy(done.at[n, v], out_ref.at[:, 128 * v:128 * v + 128], sem.at[n]).start()
-    for n in range(2):
-        pltpu.make_async_copy(done.at[n], done.at[n], sem.at[n]).wait()
+    finish(landed, sx_sem)
+    finish(slots, sr_sem)
+
+
+def combine(kept_ref, c_ref, heights_ref, resid_ref, done, sem):
+    c = [c_ref[k] for k in range(3)]
+    for v in range(4):
+        for i in range(0, kept_ref.shape[2], 8):
+            r0, u0, u1, u2, w0, w1, w2 = (kept_ref[n, v, i:i + 8] for n in range(7))
+            done[0, v, i:i + 8] = c[0] * u0 + c[1] * u1 + c[2] * u2
+            done[1, v, i:i + 8] = r0 - (c[0] * w0 + c[1] * w1 + c[2] * w2)
+        for n, out_ref in enumerate((heights_ref, resid_ref)):
+            pltpu.make_async_copy(done.at[n, v], out_ref.at[:, 128 * v:128 * v + 128], sem).start()
+    pltpu.make_async_copy(done, done, sem).wait()
 
 
 def total_any(values):
@@ -464,12 +456,12 @@
 
 
 def solution(mesh, split=SPLIT):
-    na, nb, nc = split["x"] * split["core"], split["y"], split["zh"] * split["zl"]
+    others = split["x"] * split["zh"] * split["zl"] + split["y"] * split["core"] - 2
 
     def step(*args):
         rows, cols = args[0].shape
         assert (rows, cols) == (96, 512)
-        shapes = [(16, 24, 128), (3, 16, 24, 128), (3, 16, 24, 128), (3, 8, 128)]
+        shapes = [(7, 4, rows, 128), (3, 8, 128)]
         dma = pltpu.SemaphoreType.DMA
 
         def vmem(*shape):
@@ -480,15 +472,15 @@
             functools.partial(kernel, split),
             out_shape=[jax.ShapeDtypeStruct(shape, F) for shape in shapes],
             in_specs=[pl.BlockSpec(memory_space=pltpu.HBM)] * 6,
-            out_specs=[pl.BlockSpec(memory_space=pltpu.VMEM)] * 4,
+            out_specs=[pl.BlockSpec(memory_space=pltpu.VMEM)] * 2,
             scratch_shapes=[
                 vmem(6, 4, rows, 128),
                 vmem(16, 24, 128), vmem(16, 24, 128), vmem(16, 24, 128), vmem(16, 24, 128),
                 vmem(4, 24, 128), vmem(4, 24, 128),
-                vmem(12, 8, 128), vmem(4, 8, 128), vmem(5, 8, 128), vmem(51, 8, 128),
-                vmem(2, 3, 8, 128), vmem(2, 1, 8, 128), vmem(2, 1, 8, 128), vmem(2, 12, 8, 128),
-                vmem(3, 1, 128), vmem(na, 1, 128), vmem(nb, 1, 128), vmem(nc, 1, 128),
-                dma((6,)), dma((3,)), dma((3,)), dma((3,)), dma((3,)),
+                vmem(12, 8, 128), vmem(4, 8, 128), vmem(5, 8, 128),
+                vmem(2, 3, 8, 128), vmem(2, 1, 8, 128), vmem(2, 1, 8, 128), vmem(75, 8, 128),
+                vmem(2, 1, 128), vmem(others, 1, 128),
+                dma((6,)), dma(()), dma((3,)), dma(()), dma((2,)),
             ],
             compiler_params=pltpu.CompilerParams(
                 collective_id=0, has_side_effects=True, vmem_limit_bytes=12 * 2**20
@@ -497,9 +489,9 @@
         return tuple(pl.pallas_call(
             combine,
             out_shape=[jax.ShapeDtypeStruct((rows, cols), F)] * 2,
-            in_specs=[pl.BlockSpec(memory_space=pltpu.VMEM)] * 4,
+            in_specs=[pl.BlockSpec(memory_space=pltpu.VMEM)] * 2,
             out_specs=[pl.BlockSpec(memory_space=pltpu.HBM)] * 2,
-            scratch_shapes=[vmem(2, 4, rows, 128), dma((2,))],
+            scratch_shapes=[vmem(2, 4, rows, 128), dma(())],
             compiler_params=pltpu.CompilerParams(vmem_limit_bytes=12 * 2**20),
         )(*parts))
 

time: 46 us -> 46.3 us (level); the launches traced: 45.1 us -> 46.1 us
  Pallas kernels: 44.5 us -> 45.5 us
    pallas_call x1, Pallas kernels: 43.5 us -> 44.7 us  [step(): pl.pallas_call(functools.partial(kernel, split), out_shape=[jax.ShapeDtyp...]
where the time goes in v4:
time: 46.3 us; the launch traced here: 46.1 us
  Pallas kernels  45.5 us (98%)
  between operations  0.64 us (1%)
    pallas_call x1, Pallas kernels, step(): pl.pallas_call(functools.partial(kernel, split), out_shape=[jax.ShapeDtyp...  44.7 us

profile of v4, /device:TPU:1, one launch (start us, length us, event | category | flops | bytes accessed | tf_op | source)
XLA Modules:
  0.0 46.1 jit_solution(6709062541794523860)
XLA Ops:
  0.6 44.7 %shard_map.77 = (f32[7,4,96,128]{3,2,1,0:T(8,128)S(1)}, f32[3,8,128]{2,1,0:T(8,128)S(1)}) custom-call(f32[96,512]{1,0:T(8,128)} %refs_0_.1, f32[96,512]{1,0:T(8,128)} %refs_1_.1, f32[96,512]{1,0:T(8,128)} %refs_2_.1, f32[96,512]{1,0:T(8,128)} %refs_3_.1, f32[96,512]{1,0:T(8,128)} %refs_4_.1, f32[96,512]{1,0:T(8,128)} %refs_5_.1), custom_call_target="tpu_custom_call" | custom-call | tf_op jit(solution)/shard_map/pallas_call | solution.py:471
  45.3 0.8 %shard_map.78 = (f32[96,512]{1,0:T(8,128)}, f32[96,512]{1,0:T(8,128)}) custom-call(f32[7,4,96,128]{3,2,1,0:T(8,128)S(1)} %get-tuple-element.4.kept_ref, f32[3,8,128]{2,1,0:T(8,128)S(1)} %get-tuple-element.5.c_ref), custom_call_target="tpu_custom_call" | custom-call | tf_op jit(solution)/shard_map/pallas_call | solution.py:489

commit v5 on v4

--- a/solution.py
+++ b/solution.py
@@ -59,7 +59,7 @@
     nrow, ncol = ny * nzh * ncore, nzl * nx
     inputs, refs = refs[:6], refs[6:]
     kept_ref, c_ref = refs[:2]
-    (raw, rw_ref, dw_ref, diag_ref, inv_ref, lw_ref, uw_ref,
+    (raw, rw_ref, dw_ref, diag_ref, inv_ref, lw_ref, uw_ref, u_ref, w_ref, sums_ref, coarse_ref,
      s1h, s1u, s1d, sh, su, sd, landed,
      part, slots,
      in_sem, sx_sem, gx_sem, sr_sem, gr_sem) = refs[2:]
@@ -67,16 +67,23 @@
     got1 = landed.at[pl.ds(0, 51)]
     got = [landed.at[pl.ds(51 + 12 * j, 12)] for j in range(2)]
     row, col = lax.axis_index("row"), lax.axis_index("col")
-    up, down = lax.rem(row + nrow - 1, nrow), lax.rem(row + 1, nrow)
-    left, right = lax.rem(col + ncol - 1, ncol), lax.rem(col + 1, ncol)
+
+    def wrap(k, n):
+        return jnp.where(k >= n, k - n, k)
+
+    up, down = wrap(row + nrow - 1, nrow), wrap(row + 1, nrow)
+    left, right = wrap(col + ncol - 1, ncol), wrap(col + 1, ncol)
     neighbours = [(up, left), (up, right), (down, left), (down, right), (up, col), (down, col), (row, left), (row, right)]
 
-    y, zh, core = row // (nzh * ncore), lax.rem(row // ncore, nzh), lax.rem(row, ncore)
-    zl, x = col // nx, lax.rem(col, nx)
+    half = lax.div(row, jnp.int32(ncore))
+    y, core = lax.div(row, jnp.int32(nzh * ncore)), row - half * ncore
+    zh, zl = half - y * nzh, lax.div(col, jnp.int32(nx))
+    x = col - zl * nx
     z = zh * nzl + zl
 
     def device(y, z, core, x):
-        return ((y * nzh + z // nzl) * ncore + core, lax.rem(z, nzl) * nx + x)
+        high = lax.div(z, jnp.int32(nzl))
+        return ((y * nzh + high) * ncore + core, (z - high * nzl) * nx + x)
 
     nz = nzh * nzl
 
@@ -86,8 +93,8 @@
     stage_a = sorted(((ring(i, nx) + ring(k, nz), i, k) for i in range(nx) for k in range(nz) if i or k), reverse=True)
     stage_b = sorted(((ring(k, ny), k, i) for k in range(ny) for i in range(ncore) if i or k), reverse=True)
     hops_a = [far for far, _, _ in stage_a]
-    stage_a = [device(y, lax.rem(z + k, nz), core, lax.rem(x + i, nx)) for _, i, k in stage_a]
-    stage_b = [device(lax.rem(y + k, ny), z, lax.rem(core + i, ncore), x) for _, k, i in stage_b]
+    stage_a = [device(y, wrap(z + k, nz), core, wrap(x + i, nx)) for _, i, k in stage_a]
+    stage_b = [device(wrap(y + k, ny), z, wrap(core + i, ncore), x) for _, k, i in stage_b]
 
     farther = sum(far > 5 for far in hops_a)
     partners = stage_a[:farther] + neighbours + stage_a[farther:] + stage_b
@@ -218,9 +225,16 @@
 
     pl.semaphore_wait(barrier, len(partners))
     exchange(s1h, s1u, s1d, got1, 4, 5, sx_sem, gx_sem.at[0])
-    for k in range(16):
-        rw_ref[k] = rw[k]
-        dw_ref[k] = dw[k]
+    inner = [k for k in range(16) if k >= 4 and k % 4]
+
+    @pl.when(row >= 0)
+    def _():
+        for k in range(16):
+            rw_ref[k] = rw[k]
+            dw_ref[k] = dw[k]
+        for k in inner:
+            diag_ref[k] = diag[k]
+            inv_ref[k] = 1.0 / diag[k]
 
     def assemble(own, h, v, fill=0.0):
         side = jnp.where(lane < 64, h[0], h[1])
@@ -304,10 +318,10 @@
         uw0[s] = uw0[s] + more
         diag[s] = diag[s] + more
         resid[s] = resid[s] + jnp.where(sub == 0, jnp.broadcast_to(from_up[4 + s:5 + s], shape), 0.0)
-    inv = [1.0 / d for d in diag]
     for k in range(16):
-        diag_ref[k] = diag[k]
-        inv_ref[k] = inv[k]
+        if k not in inner:
+            diag_ref[k] = diag[k]
+            inv_ref[k] = 1.0 / diag[k]
     for k in range(4):
         lw_ref[k] = lw0[k]
         uw_ref[k] = uw0[k]
@@ -330,66 +344,111 @@
         e_ends = jnp.where(
             sub8 < 4, jnp.broadcast_to(e_ends[7:8], (8, 128)), jnp.broadcast_to(e_ends[0:1], (8, 128))
         )
-        return level[:24, :128], inv_side * side + e_side, inv_ends * ends + e_ends
-
-    def operate(v, side, ends, emit):
-        west = [jnp.where(lane == 0, roll(side, -(120 + t), 1), roll(v[4 * t + 3], 1, 1)) for t in range(4)]
-        east = [jnp.where(lane == 127, roll(side, 127 - (4 + t), 1), roll(v[4 * t], -1, 1)) for t in range(4)]
-        north = [
-            jnp.where(sub == 0, jnp.broadcast_to(ends[s:s + 1], shape), roll(v[12 + s], 1, 0)) for s in range(4)
-        ]
-        south = [
-            jnp.where(sub == 23, jnp.broadcast_to(ends[4 + s:5 + s], shape), roll(v[s], -1, 0)) for s in range(4)
-        ]
+        return level, inv_side * side + e_side, inv_ends * ends + e_ends
+
+    def borders(side, ends):
+        west = [jnp.where(lane == 0, roll(side, -(120 + t), 1), 0.0) for t in range(4)]
+        east = [jnp.where(lane == 127, roll(side, 127 - (4 + t), 1), 0.0) for t in range(4)]
+        north = [jnp.where(sub == 0, jnp.broadcast_to(ends[s:s + 1], shape), 0.0) for s in range(4)]
+        south = [jnp.where(sub == 23, jnp.broadcast_to(ends[4 + s:5 + s], shape), 0.0) for s in range(4)]
+        return west, east, north, south
+
+    def operate(v, around=None):
+        west = [jnp.where(lane == 0, 0.0 if around is None else around[0][t], roll(v[4 * t + 3], 1, 1)) for t in range(4)]
+        east = [jnp.where(lane == 127, 0.0 if around is None else around[1][t], roll(v[4 * t], -1, 1)) for t in range(4)]
+        north = [jnp.where(sub == 0, 0.0 if around is None else around[2][s], roll(v[12 + s], 1, 0)) for s in range(4)]
+        south = [jnp.where(sub == 23, 0.0 if around is None else around[3][s], roll(v[s], -1, 0)) for s in range(4)]
+        image = []
         for k in range(16):
             t, s = k // 4, k % 4
             beside = (lw_ref[t] * west[t]) if s == 0 else (rw_ref[k - 1] * v[k - 1])
             beside = beside + rw_ref[k] * (east[t] if s == 3 else v[k + 1])
             beside = beside + ((uw_ref[s] * north[s]) if t == 0 else (dw_ref[k - 4] * v[k - 4]))
             beside = beside + dw_ref[k] * (south[s] if t == 3 else v[k + 4])
-            emit(k, diag_ref[k] * v[k] - beside)
+            image.append(diag_ref[k] * v[k] - beside)
+        return image
 
     def dot(a, b):
         return total([a[k] * b[k] for k in range(16)])
 
-    sums = {}
+    def fold(x):
+        return x[:8] + x[8:16] + x[16:]
+
+    order = [("g", 0), ("g", 1), ("g", 2), (0, 0), (0, 1), (0, 2), (1, 1), (1, 2), (2, 2)]
     news = ext, side, ends
-    images, fields = [], []
-    for j in range(3):
+    coarses, images = [ext[:24, :128]], [resid]
+    for j in range(2):
         if j:
             finish(got[j - 1], gx_sem.at[j])
             news = assemble(
-                coarse, [got[j - 1][3 * k:3 * k + 3].reshape(shape) for k in range(2)], [got[j - 1][6 + k] for k in range(6)]
+                coarses[j], [got[j - 1][3 * k:3 * k + 3].reshape(shape) for k in range(2)], [got[j - 1][6 + k] for k in range(6)]
             )
         level, new_side, new_ends = smooth(*news)
+        own = level[:24, :128]
         if j == 0:
-            v = [inv_ref[k] * resid[k] + level for k in range(16)]
+            v = [inv_ref[k] * resid[k] + own for k in range(16)]
             side, ends = new_side, new_ends
         else:
-            v = [inv_ref[k] * images[-1][k] + level - fields[-1][k] for k in range(16)]
+            v = [inv_ref[k] * images[j][k] + own - u_ref[0, k] for k in range(16)]
             side, ends = new_side - side, new_ends - ends
-        image = [None] * 16
-
-        def emit(k, value):
-            image[k] = value
-
-        operate(v, side, ends, emit)
-        fields.append(v)
+        image = operate(v, borders(side, ends))
         images.append(image)
-        if j < 2:
-            coarse = total(image)
-            pack(coarse, image, sh.at[j], su.at[j], sd.at[j])
-            exchange(sh.at[j], su.at[j], sd.at[j], got[j], 1, 1, sx_sem, gx_sem.at[j + 1])
-        sums["g", j] = dot(resid, v)
-        for i in range(j + 1):
-            sums[i, j] = dot(images[i], v)
-
-    order = [("g", 0), ("g", 1), ("g", 2), (0, 0), (0, 1), (0, 2), (1, 1), (1, 2), (2, 2)]
+        coarses.append(total(image))
+        pack(coarses[-1], image, sh.at[j], su.at[j], sd.at[j])
+        exchange(sh.at[j], su.at[j], sd.at[j], got[j], 1, 1, sx_sem, gx_sem.at[j + 1])
+        for k in range(16):
+            u_ref[j, k] = v[k]
+            w_ref[j, k] = image[k]
+
+        @pl.when(row >= 0)
+        def _():
+            v = [u_ref[j, k] for k in range(16)]
+            sums_ref[order.index(("g", j))] = fold(dot(resid, v))
+            for i in range(j + 1):
+                sums_ref[order.index((i, j))] = fold(dot([w_ref[i, k] for k in range(16)], v))
+            if j == 1:
+                last = [w_ref[1, k] for k in range(16)]
+                p = [inv_ref[k] * last[k] - v[k] for k in range(16)]
+                image = operate(p)
+                for k in range(16):
+                    u_ref[2, k] = p[k]
+                sums_ref[2] = fold(dot(resid, p))
+                sums_ref[5] = fold(dot([w_ref[0, k] for k in range(16)], p))
+                sums_ref[7] = fold(dot(last, p))
+                sums_ref[8] = fold(dot(image, p))
+                coarse_ref[...] = total(image)
+
+    finish(got[1], gx_sem.at[2])
+    ext, new_side, new_ends = assemble(
+        coarses[2], [got[1][3 * k:3 * k + 3].reshape(shape) for k in range(2)], [got[1][6 + k] for k in range(6)]
+    )
+    p_side, p_ends = inv_side * new_side - side, inv_ends * new_ends - ends
+    level, new_side, new_ends = smooth(ext, new_side, new_ends)
+    side, ends = new_side - side, new_ends - ends
+    own = level[:24, :128]
+    beside = cr * roll(level, -1, 1) + roll(cr * level, 1, 1) + cd * roll(level, -1, 0) + roll(cd * level, 1, 0)
+    c_image = (cdiag * level - beside)[:24, :128]
+    cross, power = [], []
+    west, east, north, south = borders(p_side, p_ends)
+    for q in range(4):
+        for weight, beyond, k in (
+            (lw_ref[q], west[q], 4 * q), (rw_ref[4 * q + 3], east[q], 4 * q + 3),
+            (uw_ref[q], north[q], q), (dw_ref[12 + q], south[q], 12 + q),
+        ):
+            flow = weight * beyond
+            cross.append(flow)
+            power.append(flow * u_ref[2, k])
+    p_image = coarse_ref[...] - total(cross)
+    sums = {name: sums_ref[k] for k, name in enumerate(order)}
+    sums["g", 2] = sums["g", 2] + fold(coarses[0] * own)
+    sums[0, 2] = sums[0, 2] + fold(coarses[1] * own)
+    sums[1, 2] = sums[1, 2] + fold(coarses[2] * own)
+    sums[2, 2] = sums[2, 2] + fold((c_image + 2.0 * p_image) * own - total(power))
+
     sums_row = jnp.zeros((1, 128), F)
     lane1 = iota((1, 128), 1)
     for k, name in enumerate(order):
         x8 = sums[name]
-        x8 = x8[:8] + x8[8:16] + x8[16:]
         for shift in (64, 32, 16, 8):
             x8 = x8 + roll(x8, shift, 1)
         one = jnp.sum(x8, axis=0, keepdims=True)
@@ -407,8 +466,19 @@
             pltpu.make_async_remote_copy(
                 part.at[stage], slots.at[base + k], sr_sem, gr_sem.at[stage], device_id=who, device_id_type=MESH
             ).start()
-        for n in range(4) if stage == 0 else range(4, 7):
-            keep(n, resid if n == 0 else (fields[n - 1] if n < 4 else images[n - 4]))
+
+        @pl.when(row >= 0)
+        def _():
+            if stage == 0:
+                v = [u_ref[2, k] + own for k in range(16)]
+                keep(3, v)
+                keep(6, operate(v, borders(side, ends)))
+            else:
+                keep(0, resid)
+                for j in range(2):
+                    keep(1 + j, [u_ref[j, k] for k in range(16)])
+                    keep(4 + j, [w_ref[j, k] for k in range(16)])
+
         finish(slots.at[pl.ds(base, len(others))], gr_sem.at[stage])
         sums_row = total_any([sums_row] + [slots[base + k] for k in range(len(others))])
         base += len(others)
@@ -477,6 +547,7 @@
                 vmem(6, 4, rows, 128),
                 vmem(16, 24, 128), vmem(16, 24, 128), vmem(16, 24, 128), vmem(16, 24, 128),
                 vmem(4, 24, 128), vmem(4, 24, 128),
+                vmem(3, 16, 24, 128), vmem(2, 16, 24, 128), vmem(9, 8, 128), vmem(24, 128),
                 vmem(12, 8, 128), vmem(4, 8, 128), vmem(5, 8, 128),
                 vmem(2, 3, 8, 128), vmem(2, 1, 8, 128), vmem(2, 1, 8, 128), vmem(75, 8, 128),
                 vmem(2, 1, 128), vmem(others, 1, 128),

time: 46.3 us -> 45.3 us (0.978)
  Pallas kernels: 45.5 us -> 44.5 us
    pallas_call x1, Pallas kernels: 44.7 us -> 43.7 us  [step(): pl.pallas_call(functools.partial(kernel, split), out_shape=[jax.ShapeDtyp...]
where the time goes in v5:
time: 45.3 us; the launch traced here: 45.1 us
  Pallas kernels  44.5 us (98%)
  between operations  0.64 us (1%)
    pallas_call x1, Pallas kernels, step(): pl.pallas_call(functools.partial(kernel, split), out_shape=[jax.ShapeDtyp...  43.7 us

profile of v5, /device:TPU:1, one launch (start us, length us, event | category | flops | bytes accessed | tf_op | source)
XLA Modules:
  0.0 45.1 jit_solution(1817089476402363723)
XLA Ops:
  0.6 43.7 %shard_map.77 = (f32[7,4,96,128]{3,2,1,0:T(8,128)S(1)}, f32[3,8,128]{2,1,0:T(8,128)S(1)}) custom-call(f32[96,512]{1,0:T(8,128)} %refs_0_.1, f32[96,512]{1,0:T(8,128)} %refs_1_.1, f32[96,512]{1,0:T(8,128)} %refs_2_.1, f32[96,512]{1,0:T(8,128)} %refs_3_.1, f32[96,512]{1,0:T(8,128)} %refs_4_.1, f32[96,512]{1,0:T(8,128)} %refs_5_.1), custom_call_target="tpu_custom_call" | custom-call | tf_op jit(solution)/shard_map/pallas_call | solution.py:541
  44.3 0.8 %shard_map.78 = (f32[96,512]{1,0:T(8,128)}, f32[96,512]{1,0:T(8,128)}) custom-call(f32[7,4,96,128]{3,2,1,0:T(8,128)S(1)} %get-tuple-element.4.kept_ref, f32[3,8,128]{2,1,0:T(8,128)S(1)} %get-tuple-element.5.c_ref), custom_call_target="tpu_custom_call" | custom-call | tf_op jit(solution)/shard_map/pallas_call | solution.py:560

commit v6 on v5

--- a/solution.py
+++ b/solution.py
@@ -460,7 +460,7 @@
                 kept_ref[n, v, pl.ds(t, 24, stride=4), :] = value
 
     base = 0
-    for stage, others in enumerate((stage_a, stage_b)):
+    for stage, others in enumerate((stage_b, stage_a)):
         part[stage] = sums_row
         for k, who in enumerate(others):
             pltpu.make_async_remote_copy(

time: 45.3 us -> 44.7 us (0.987)
  Pallas kernels: 44.5 us -> 43.9 us
    pallas_call x1, Pallas kernels: 43.7 us -> 43.2 us  [step(): pl.pallas_call(functools.partial(kernel, split), out_shape=[jax.ShapeDtyp...]
where the time goes in v6:
time: 44.7 us; the launch traced here: 44.6 us
  Pallas kernels  43.9 us (98%)
  between operations  0.64 us (1%)
    pallas_call x1, Pallas kernels, step(): pl.pallas_call(functools.partial(kernel, split), out_shape=[jax.ShapeDtyp...  43.2 us

profile of v6, /device:TPU:1, one launch (start us, length us, event | category | flops | bytes accessed | tf_op | source)
XLA Modules:
  0.0 44.6 jit_solution(11893359953556917709)
XLA Ops:
  0.6 43.2 %shard_map.77 = (f32[7,4,96,128]{3,2,1,0:T(8,128)S(1)}, f32[3,8,128]{2,1,0:T(8,128)S(1)}) custom-call(f32[96,512]{1,0:T(8,128)} %refs_0_.1, f32[96,512]{1,0:T(8,128)} %refs_1_.1, f32[96,512]{1,0:T(8,128)} %refs_2_.1, f32[96,512]{1,0:T(8,128)} %refs_3_.1, f32[96,512]{1,0:T(8,128)} %refs_4_.1, f32[96,512]{1,0:T(8,128)} %refs_5_.1), custom_call_target="tpu_custom_call" | custom-call | tf_op jit(solution)/shard_map/pallas_call | solution.py:541
  43.8 0.8 %shard_map.78 = (f32[96,512]{1,0:T(8,128)}, f32[96,512]{1,0:T(8,128)}) custom-call(f32[7,4,96,128]{3,2,1,0:T(8,128)S(1)} %get-tuple-element.4.kept_ref, f32[3,8,128]{2,1,0:T(8,128)S(1)} %get-tuple-element.5.c_ref), custom_call_target="tpu_custom_call" | custom-call | tf_op jit(solution)/shard_map/pallas_call | solution.py:560
